TPU v7x, 512 devices: a whole 4x4x16 slice. The times are simulated.
512 devices in a mesh: hist: 16 (over y, x_hi, core), item: 32 (over z, x_lo).
Axes of the slice: x: 4 (x_hi: 2, x_lo: 2; x = x_hi * 2 + x_lo), y: 4, z: 16, core: 2. Of those that a mesh axis runs over, the one named last changes fastest.
Arguments:
- events: bfloat16 [32, 16384, 512], P('item', 'hist'), may hold values from -6 to 6
- item_ids: int32 [32, 16384], P('item', 'hist'), may hold values from 0 to 524287
- lengths: int32 [32], P('item'), may hold values from 4096 to 16384, as said below
- w_proj: bfloat16 [512, 2048], replicated, may hold values from -0.25 to 0.25
- w_out: bfloat16 [512, 512], replicated, may hold values from -0.25 to 0.25
- repeat_bias: float32 [4], replicated, may hold values from 1 to 3
- item_slab: bfloat16 [524288, 512], P(('hist', 'item')), as said below
Outputs:
- log_probs: float32 [32, 524288], P(None, ('hist', 'item'))
Inputs may be any that keep to these rules, and one draw needn't show every extreme that they name: `lengths`: some user's history is fully valid in every draw. `item_slab`: entries lie within -240 / sqrt(512) and 240 / sqrt(512).
All inputs are finite; a program needn't handle non-finite values.
Results may differ from a plain program's by a relative error of at most 0.00075.
Values may be sent and summed in bfloat16 or wider, within the bound.
No kernel may reach another device: no remote copies, remote signals or barrier semaphores. Data moves between devices by JAX's collectives and lax.ppermute only.
A program may use at most 64 MiB of HBM per device.

v0:
```python
import math

import jax
import jax.numpy as jnp
from jax import lax
from jax.sharding import PartitionSpec as P

WINDOW = 1024


def shifted(block, axis, distance):
    devices = range(lax.axis_size(axis))
    route = [(i - distance, i) for i in devices if i - distance in devices]
    return lax.ppermute(block, axis, route)


def take_rows(array, user_index, first_row, rows):
    starts = (user_index, first_row) + (0,) * (array.ndim - 2)
    sizes = (1, rows) + tuple(array.shape[2:])
    return lax.dynamic_slice(array, starts, sizes)[0]


def row_normed(pooled):
    return (pooled * lax.rsqrt(jnp.mean(pooled * pooled, axis=1, keepdims=True) + 1e-06)).astype(
        jnp.bfloat16
    )


def local(events, item_ids, lengths, w_proj, w_out, repeat_bias, item_slab):
    users_dev, local_len, model_width = events.shape
    head_count = repeat_bias.shape[0]
    head_dim = model_width // head_count
    block_rows = min(256, local_len)
    block_count = local_len // block_rows
    projected = jax.nn.silu(
        jnp.einsum("uld,de->ule", events, w_proj, preferred_element_type=jnp.float32)
    ).astype(jnp.bfloat16)
    gate_part = projected[:, :, :model_width]
    value_part = projected[:, :, model_width : 2 * model_width]
    query_part = projected[:, :, 2 * model_width : 3 * model_width]
    key_part = projected[:, :, 3 * model_width :]
    tail_pairs = jnp.concatenate([key_part, value_part], axis=2)
    received = shifted(tail_pairs, "hist", 1)
    halo_ids = shifted(item_ids, "hist", 1)
    key_cat = jnp.concatenate([received[:, :, :model_width], key_part], axis=1)
    value_cat = jnp.concatenate([received[:, :, model_width:], value_part], axis=1)
    id_cat = jnp.concatenate([halo_ids, item_ids], axis=1)
    pos_offset = lax.axis_index("hist") * local_len
    scale = 1.0 / math.sqrt(head_dim)

    def one_block(flat_index):
        user_index = flat_index // block_count
        first_row = flat_index % block_count * block_rows
        length = lengths[user_index]
        queries = take_rows(query_part, user_index, first_row, block_rows).reshape(
            block_rows, head_count, head_dim
        )
        key_rows = take_rows(key_cat, user_index, first_row, block_rows + WINDOW).reshape(
            block_rows + WINDOW, head_count, head_dim
        )
        value_rows = take_rows(value_cat, user_index, first_row, block_rows + WINDOW).reshape(
            block_rows + WINDOW, head_count, head_dim
        )
        query_ids = take_rows(item_ids, user_index, first_row, block_rows)
        key_ids = take_rows(id_cat, user_index, first_row, block_rows + WINDOW)
        scores = (
            jnp.einsum("qhd,khd->hqk", queries, key_rows, preferred_element_type=jnp.float32)
            * scale
        )
        same_item = (query_ids[:, None] == key_ids[None, :]).astype(jnp.float32)
        scores = scores + repeat_bias[:, None, None] * same_item[None]
        row_index = jnp.arange(block_rows, dtype=jnp.int32)[:, None]
        col_index = jnp.arange(block_rows + WINDOW, dtype=jnp.int32)[None, :]
        key_pos = pos_offset + first_row + col_index - WINDOW
        valid_mask = (
            (col_index >= row_index + 1)
            & (col_index <= row_index + WINDOW)
            & (key_pos >= 0)
            & (key_pos < length)
        )
        weights = (jnp.where(valid_mask[None], jax.nn.silu(scores), 0.0) / WINDOW).astype(
            jnp.bfloat16
        )
        mixed = jnp.einsum(
            "hqk,khd->qhd", weights, value_rows, preferred_element_type=jnp.float32
        ).reshape(block_rows, model_width)
        centered = mixed - jnp.mean(mixed, axis=1, keepdims=True)
        normed = centered * lax.rsqrt(jnp.mean(centered * centered, axis=1, keepdims=True) + 1e-06)
        gate_rows = take_rows(gate_part, user_index, first_row, block_rows)
        gated_rows = (normed * gate_rows.astype(jnp.float32)).astype(jnp.bfloat16)
        x_block = take_rows(events, user_index, first_row, block_rows)
        layer_out = jnp.dot(gated_rows, w_out, preferred_element_type=jnp.float32) + x_block.astype(
            jnp.float32
        )
        query_pos = pos_offset + first_row + jnp.arange(block_rows, dtype=jnp.int32)
        return jnp.sum(jnp.where((query_pos < length)[:, None], layer_out, 0.0), axis=0)

    partial_sums = lax.map(one_block, jnp.arange(users_dev * block_count, dtype=jnp.int32))
    partial_sums = jnp.sum(partial_sums.reshape(users_dev, block_count, model_width), axis=1)
    pooled = lax.psum(partial_sums, "hist")
    user_vecs = lax.all_gather(row_normed(pooled), "item", axis=0, tiled=True)
    logits = 4.0 * jnp.einsum("bd,vd->bv", user_vecs, item_slab, preferred_element_type=jnp.float32)
    top_logit = lax.pmax(jnp.max(logits, axis=1), ("hist", "item"))
    exp_total = lax.psum(jnp.sum(jnp.exp(logits - top_logit[:, None]), axis=1), ("hist", "item"))
    return logits - (top_logit + jnp.log(exp_total))[:, None]


def solution(mesh):
    placed = (
        P("item", "hist", None),
        P("item", "hist"),
        P("item"),
        P(),
        P(),
        P(),
        P(("hist", "item"), None),
    )
    return jax.shard_map(
        local, mesh=mesh, in_specs=placed, out_specs=P(None, ("hist", "item")), check_vma=False
    )
```

profile of v0, /device:TPU:1, one launch (start us, length us, event | category | flops | bytes accessed | tf_op | source)
XLA Modules:
  0.0 428.6 jit_solution(7137822212186388920)
XLA Ops:
  0.0 1.6 copy-done
  1.6 4.2 fusion.16
  5.8 1.8 fusion.21
  7.6 1.7 pad_maximum_fusion
  9.3 6.0 %collective-permute-start = (bf16[1,1024,1024]{2,1,0:T(8,128)(2,1)}, bf16[1,1024,1024]{2,1,0:T(8,128)(2,1)}, u32[]{:S(2)}, u32[]{:S(2)}) collective-permute-start(bf16[1,1024,1024]{2,1,0:T(8,128)(2,1)} %pad_maximum_fusion), channel_id=1, source_target_pairs={{0,32},{32,64},{64,96},{96,128},{128,160},{160,192},{192,224},{224... | collective-permute-start | bytes 6291464 | tf_op jit(solution)/shard_map/ppermute | solution.py:14
  15.3 1.9 collective-permute-start.1
  17.3 21.3 %collective-permute-done.1 = s32[1,1024]{1,0:T(1,128)S(1)} collective-permute-done((s32[1,1024]{1,0:T(1,128)S(1)}, s32[1,1024]{1,0:T(1,128)S(1)}, u32[]{:S(2)}, u32[]{:S(2)}) %collective-permute-start.1) | collective-permute-done | bytes 4128 | tf_op jit(solution)/shard_map/ppermute | solution.py:14
  38.6 1.8 fusion.22
  40.4 2.2 pad_maximum_fusion.1
  42.6 82.6 %while.12 = (s32[]{:T(128)}, f32[4,512]{1,0:T(4,128)S(1)}, s32[4]{0:T(128)S(1)}, s32[]{:T(128)}, s32[1]{0:T(128)}, /*index=5*/bf16[1,2048,512]{2,1,0:T(8,128)(2,...) while((s32[]{:T(128)}, f32[4,512]{1,0:T(4,128)S(1)}, ...), condition=%wide.region_4.5_spmd, body=%wide.region_0.4_spmd.sunk | while | flops 822417152 | bytes 21932992 | solution.py:98
  45.1 3.0 constant_dynamic-slice_fusion.8
  48.1 2.4 copy.45
  50.5 1.5 copy.47
  52.0 1.2 compare_convert_fusion.2
  53.2 1.1 constant_dynamic-slice_fusion.9
  54.4 0.7 fusion.47
  55.7 5.0 %fusion.49 = (f32[256]{0:T(256)S(1)}, f32[4,128,256]{2,1,0:T(8,128)S(1)}) fusion(bf16[1280,4,128]{0,2,1:T(8,128)(2,1)} %bitcast.78, bf16[256,4,128]{0,2,1:T(8,128)(2,1)S(1)} %bitcast.80, bf16[1280,4,128]{0,2,1:T(8,128)(2,1)} %bitcast.79, f32[256,1280]{1,0:T(8,128)} %compare_convert_fusion.2, f32[4]{0:T(128)S(1)} %get-tuple-element.440, ...), kind=kOutput, calls=%fused_computation.51.clone.1 | convolution fusion | flops 684326656 | bytes 5047312 | tf_op jit(solution)/shard_map/while/body/eval_jaxpr/hqk,khd->qhd/dot_general | solution.py:84
  61.8 1.5 fusion.52
  65.7 3.0 constant_dynamic-slice_fusion.8
  68.7 2.4 copy.45
  71.2 1.5 copy.47
  72.6 1.2 compare_convert_fusion.2
  73.9 1.1 constant_dynamic-slice_fusion.9
  75.1 0.7 fusion.47
  76.4 5.0 %fusion.49 = (f32[256]{0:T(256)S(1)}, f32[4,128,256]{2,1,0:T(8,128)S(1)}) fusion(bf16[1280,4,128]{0,2,1:T(8,128)(2,1)} %bitcast.78, bf16[256,4,128]{0,2,1:T(8,128)(2,1)S(1)} %bitcast.80, bf16[1280,4,128]{0,2,1:T(8,128)(2,1)} %bitcast.79, f32[256,1280]{1,0:T(8,128)} %compare_convert_fusion.2, f32[4]{0:T(128)S(1)} %get-tuple-element.440, ...), kind=kOutput, calls=%fused_computation.51.clone.1 | convolution fusion | flops 684326656 | bytes 5047312 | tf_op jit(solution)/shard_map/while/body/eval_jaxpr/hqk,khd->qhd/dot_general | solution.py:84
  82.4 1.5 fusion.52
  86.4 3.0 constant_dynamic-slice_fusion.8
  89.4 2.4 copy.45
  91.8 1.5 copy.47
  93.3 1.2 compare_convert_fusion.2
  94.5 1.1 constant_dynamic-slice_fusion.9
  95.7 0.7 fusion.47
  97.0 5.0 %fusion.49 = (f32[256]{0:T(256)S(1)}, f32[4,128,256]{2,1,0:T(8,128)S(1)}) fusion(bf16[1280,4,128]{0,2,1:T(8,128)(2,1)} %bitcast.78, bf16[256,4,128]{0,2,1:T(8,128)(2,1)S(1)} %bitcast.80, bf16[1280,4,128]{0,2,1:T(8,128)(2,1)} %bitcast.79, f32[256,1280]{1,0:T(8,128)} %compare_convert_fusion.2, f32[4]{0:T(128)S(1)} %get-tuple-element.440, ...), kind=kOutput, calls=%fused_computation.51.clone.1 | convolution fusion | flops 684326656 | bytes 5047312 | tf_op jit(solution)/shard_map/while/body/eval_jaxpr/hqk,khd->qhd/dot_general | solution.py:84
  103.0 1.5 fusion.52
  107.0 3.0 constant_dynamic-slice_fusion.8
  110.0 2.4 copy.45
  112.5 1.5 copy.47
  113.9 1.2 compare_convert_fusion.2
  115.2 1.1 constant_dynamic-slice_fusion.9
  116.4 0.7 fusion.47
  117.7 5.0 %fusion.49 = (f32[256]{0:T(256)S(1)}, f32[4,128,256]{2,1,0:T(8,128)S(1)}) fusion(bf16[1280,4,128]{0,2,1:T(8,128)(2,1)} %bitcast.78, bf16[256,4,128]{0,2,1:T(8,128)(2,1)S(1)} %bitcast.80, bf16[1280,4,128]{0,2,1:T(8,128)(2,1)} %bitcast.79, f32[256,1280]{1,0:T(8,128)} %compare_convert_fusion.2, f32[4]{0:T(128)S(1)} %get-tuple-element.440, ...), kind=kOutput, calls=%fused_computation.51.clone.1 | convolution fusion | flops 684326656 | bytes 5047312 | tf_op jit(solution)/shard_map/while/body/eval_jaxpr/hqk,khd->qhd/dot_general | solution.py:84
  123.7 1.5 fusion.52
  125.2 34.1 %psum.14 = f32[1,512]{1,0:T(1,128)S(1)} all-reduce(f32[1,512]{1,0:T(1,128)S(1)} %bitcast.83), channel_id=1, replica_groups=mesh['hist'=16,'item'=32] {'hist'}, use_global_device_ids=true, to_apply=%region_6.7 | all-reduce | flops 512 | bytes 4096 | tf_op jit(solution)/shard_map/psum | solution.py:100
  160.6 54.2 %all-gather = bf16[32,1,512]{2,1,0:T(2,128)(2,1)S(1)} all-gather(bf16[1,1,512]{2,1,0:T(2,128)(2,1)S(1)} %convert_bitcast_fusion), channel_id=1, replica_groups=mesh['hist'=16,'item'=32] {'item'}, dimensions={0}, use_global_device_ids=true | all-gather | bytes 33792 | tf_op jit(solution)/shard_map/all_gather | solution.py:101
  214.8 1.7 fusion.23
  216.6 110.7 %pmax.7 = f32[32]{0:T(128)S(1)} all-reduce(f32[32]{0:T(128)S(1)} %get-tuple-element.281), channel_id=1, replica_groups=mesh['hist'=16,'item'=32] {'hist','item'}, use_global_device_ids=true, to_apply=%region_9.10 | all-reduce | flops 32 | bytes 256 | tf_op jit(solution)/shard_map/pmax | solution.py:103
  327.4 100.4 %psum.15 = f32[32]{0:T(128)S(1)} all-reduce(f32[32]{0:T(128)S(1)} %exponential_reduce_fusion), channel_id=1, replica_groups=mesh['hist'=16,'item'=32] {'hist','item'}, use_global_device_ids=true, to_apply=%region_11.12 | all-reduce | flops 32 | bytes 256 | tf_op jit(solution)/shard_map/psum | solution.py:104
  427.8 0.7 broadcast_subtract_fusion
  (70 shorter events, 10.6 us)
Async XLA Ops:
  0.0 1.6 copy-start
  7.6 1.7 copy-start.1
  7.6 7.7 %copy-start.3 = (s32[1,1024]{1,0:T(1,128)S(1)}, s32[1,1024]{1,0:T(1,128)}, u32[]{:S(2)}) copy-start(s32[1,1024]{1,0:T(1,128)} %param.10) | copy-start | bytes 12292
  9.3 29.3 %collective-permute-start = (bf16[1,1024,1024]{2,1,0:T(8,128)(2,1)}, bf16[1,1024,1024]{2,1,0:T(8,128)(2,1)}, u32[]{:S(2)}, u32[]{:S(2)}) collective-permute-start(bf16[1,1024,1024]{2,1,0:T(8,128)(2,1)} %pad_maximum_fusion), channel_id=1, source_target_pairs={{0,32},{32,64},{64,96},{96,128},{128,160},{160,192},{192,224},{224... | collective-permute-start | bytes 6291464 | tf_op jit(solution)/shard_map/ppermute | solution.py:14
  15.3 23.3 %collective-permute-start.1 = (s32[1,1024]{1,0:T(1,128)S(1)}, s32[1,1024]{1,0:T(1,128)S(1)}, u32[]{:S(2)}, u32[]{:S(2)}) collective-permute-start(s32[1,1024]{1,0:T(1,128)S(1)} %copy-done.3), channel_id=1, source_target_pairs={{0,32},{32,64},{64,96},{96,128},{128,160},{160,192},{192,224},{224... | collective-permute-start | bytes 12296 | tf_op jit(solution)/shard_map/ppermute | solution.py:14
  38.6 1.9 copy-start.2
  40.4 2.2 copy-start.4
where the time goes:
time: 430 us; the launch traced here: 429 us
  blocking collectives  299 us (70%)
  local copies, waits for them, and re-layouts  40.7 us (9%)
  matrix products  31.8 us (7%)
  waiting for transfers between devices  21.3 us (5%)
  other arithmetic  18.8 us (4%)
  starting transfers between devices  7.95 us (2%)
  loops' own time  7.86 us (2%)
    pmax x1, blocking collectives, local(): top_logit = lax.pmax(jnp.max(logits, axis=1), ('hist', 'item'))  111 us
    psum x1, blocking collectives, local(): lax.psum(jnp.sum(jnp.exp(logits - top_logit[:, None]), axis=1), ('hist',...  100 us
    all_gather x1, blocking collectives, local(): user_vecs = lax.all_gather(row_normed(pooled), 'item', axis=0, tiled=True)  54.2 us
    psum x1, blocking collectives, local(): pooled = lax.psum(partial_sums, 'hist')  34.1 us
    dynamic_slice x32, local copies, waits for them, and re-layouts, take_rows(): return lax.dynamic_slice(array, starts, sizes)[0]  32.9 us
    ppermute x2, waiting for transfers between devices, shifted(): return lax.ppermute(block, axis, route)  21.3 us
    dot_general x4, matrix products, one_block(): jnp.einsum('hqk,khd->qhd', weights, value_rows, preferred_element_type=jn...  20.1 us
  transfers between devices with their start and end apart: 2, of which 1 were waited for; matrix products, arithmetic and copies ran while one was open for 0% of the time, Pallas kernels for 0%

commit v1 on v0

v1 whole, which is shorter than its diff:
```python
import functools
import math

import jax
import jax.numpy as jnp
from jax import lax
from jax.experimental import pallas as pl
from jax.experimental.pallas import tpu as pltpu
from jax.sharding import PartitionSpec as P

WINDOW = 1024
BLOCK = 256
NT = (((1,), (1,)), ((), ()))


def mm(a, b):
    return jnp.dot(a, b, preferred_element_type=jnp.float32)


def silu(x):
    half = 0.5 * x
    return half * jnp.tanh(half) + half


def spread_ids(ids_ref, out_ref):
    for b in range(out_ref.shape[0] // 128):
        row = ids_ref[:, b * 128 : (b + 1) * 128]
        out_ref[b * 128 : (b + 1) * 128, :] = jnp.broadcast_to(row, (128, 128)).T


def positions(first):
    return first + lax.broadcasted_iota(jnp.int32, (BLOCK, 1), 0)


def one_chunk(q, k, qid, kid, bias, keep):
    half = lax.dot_general(q, k, NT, preferred_element_type=jnp.float32)
    same = jnp.concatenate([qid] * (BLOCK // 128), axis=1) == kid
    half = half + jnp.where(same, bias, 0.0)
    weights = half * jnp.tanh(half) + half
    if keep is not None:
        weights = jnp.where(keep, weights, 0.0)
    return weights.astype(jnp.bfloat16)


def own_kernel(meta, bias_ref, x_ref, w_ref, ids_ref, gate_ref, q_ref, part_ref, k_buf, v_buf, qid_buf):
    rows, width = x_ref.shape
    heads = q_ref.shape[0]
    hd = width // heads
    length, start = meta[0], meta[1]
    scale = 0.5 / math.sqrt(hd)
    spread_ids(ids_ref, qid_buf)
    for r in range(rows // BLOCK):
        rs = slice(r * BLOCK, (r + 1) * BLOCK)
        x = x_ref[rs, :]
        gate_ref[rs, :] = silu(mm(x, w_ref[:, :width])).astype(jnp.bfloat16)
        pos = positions(start + r * BLOCK)
        v = jnp.where(pos < length, silu(mm(x, w_ref[:, width : 2 * width])), 0.0).astype(jnp.bfloat16)
        q = silu(mm(x, w_ref[:, 2 * width : 3 * width])).astype(jnp.bfloat16).astype(jnp.float32) * scale
        q = q.astype(jnp.bfloat16)
        k = silu(mm(x, w_ref[:, 3 * width :])).astype(jnp.bfloat16)
        for h in range(heads):
            cs = slice(h * hd, (h + 1) * hd)
            v_buf[h, rs, :] = v[:, cs]
            q_ref[h, rs, :] = q[:, cs]
            k_buf[h, rs, :] = k[:, cs]
    row = lax.broadcasted_iota(jnp.int32, (BLOCK, BLOCK), 0)
    col = lax.broadcasted_iota(jnp.int32, (BLOCK, BLOCK), 1)

    def head(h, carry):
        bias = 0.5 * bias_ref[h]
        for r in range(rows // BLOCK):
            rs = slice(r * BLOCK, (r + 1) * BLOCK)
            q, qid = q_ref[h, rs, :], qid_buf[rs, :]
            acc = None
            for c in range(r + 1):
                cs = slice(c * BLOCK, (c + 1) * BLOCK)
                weights = one_chunk(
                    q, k_buf[h, cs, :], qid, ids_ref[:, cs], bias, col <= row if c == r else None
                )
                term = mm(weights, v_buf[h, cs, :])
                acc = term if acc is None else acc + term
            part_ref[h, rs, :] = acc
        return carry

    lax.fori_loop(0, heads, head, 0)


def halo_kernel(
    meta, bias_ref, x_ref, w_ref, ids_ref, own_ids_ref, events_ref, gate_ref, q_ref, part_ref, w_out_ref,
    out_ref, k_buf, v_buf, qid_buf, mix_buf, gated_buf,
):
    rows, width = x_ref.shape
    heads = q_ref.shape[0]
    hd = width // heads
    length, start = meta[0], meta[1]
    spread_ids(own_ids_ref, qid_buf)
    for r in range(rows // BLOCK):
        rs = slice(r * BLOCK, (r + 1) * BLOCK)
        x = x_ref[rs, :]
        pos = positions(start - WINDOW + r * BLOCK)
        v = silu(mm(x, w_ref[:, width : 2 * width]))
        v = jnp.where((pos >= 0) & (pos < length), v, 0.0).astype(jnp.bfloat16)
        k = silu(mm(x, w_ref[:, 3 * width :])).astype(jnp.bfloat16)
        for h in range(heads):
            cs = slice(h * hd, (h + 1) * hd)
            v_buf[h, rs, :] = v[:, cs]
            k_buf[h, rs, :] = k[:, cs]
    row = lax.broadcasted_iota(jnp.int32, (BLOCK, BLOCK), 0)
    col = lax.broadcasted_iota(jnp.int32, (BLOCK, BLOCK), 1)

    def head(h, carry):
        bias = 0.5 * bias_ref[h]
        for r in range(rows // BLOCK):
            rs = slice(r * BLOCK, (r + 1) * BLOCK)
            q, qid = q_ref[h, rs, :], qid_buf[rs, :]
            acc = part_ref[h, rs, :]
            for c in range(r, rows // BLOCK):
                cs = slice(c * BLOCK, (c + 1) * BLOCK)
                weights = one_chunk(
                    q, k_buf[h, cs, :], qid, ids_ref[:, cs], bias, col > row if c == r else None
                )
                acc = acc + mm(weights, v_buf[h, cs, :])
            mix_buf[h, rs, :] = acc
        return carry

    lax.fori_loop(0, heads, head, 0)
    for r in range(rows // BLOCK):
        rs = slice(r * BLOCK, (r + 1) * BLOCK)
        mixed = jnp.concatenate([mix_buf[h, rs, :] for h in range(heads)], axis=1)
        centered = mixed - jnp.mean(mixed, axis=1, keepdims=True)
        spread = jnp.mean(centered * centered, axis=1, keepdims=True)
        normed = centered * lax.rsqrt(spread + 1e-06 * WINDOW * WINDOW)
        gated_buf[rs, :] = (normed * gate_ref[rs, :].astype(jnp.float32)).astype(jnp.bfloat16)
    place = start + lax.broadcasted_iota(jnp.int32, (8, rows), 1)
    counted = jnp.where(place < length, 1.0, 0.0).astype(jnp.bfloat16)
    gated_sum = mm(counted, gated_buf[...])
    event_sum = mm(counted, events_ref[...])
    projected = jnp.dot(
        gated_sum, w_out_ref[...].astype(jnp.float32),
        preferred_element_type=jnp.float32, precision=lax.Precision.HIGHEST,
    )
    total = (projected + event_sum)[:1]
    for j in range(out_ref.shape[0]):
        out_ref[j] = total


SMEM = pl.BlockSpec(memory_space=pltpu.SMEM)
VMEM = pl.BlockSpec(memory_space=pltpu.VMEM)


def own_part(meta, bias, x, w, ids):
    rows, width = x.shape
    heads = bias.shape[0]
    hd = width // heads
    return pl.pallas_call(
        own_kernel,
        out_shape=(
            jax.ShapeDtypeStruct((rows, width), jnp.bfloat16),
            jax.ShapeDtypeStruct((heads, rows, hd), jnp.bfloat16),
            jax.ShapeDtypeStruct((heads, rows, hd), jnp.float32),
        ),
        in_specs=[SMEM, SMEM, VMEM, VMEM, VMEM],
        out_specs=(VMEM, VMEM, VMEM),
        scratch_shapes=[
            pltpu.VMEM((heads, rows, hd), jnp.bfloat16),
            pltpu.VMEM((heads, rows, hd), jnp.bfloat16),
            pltpu.VMEM((rows, 128), jnp.int32),
        ],
        compiler_params=pltpu.CompilerParams(vmem_limit_bytes=24 << 20),
        cost_estimate=pl.CostEstimate(flops=8 * 10**9, bytes_accessed=10**7, transcendentals=4 * 10**6),
        name="own_part",
    )(meta, bias, x, w, ids)


def halo_part(copies, meta, bias, halo, w, halo_ids, ids, x, gate, q, part, w_out):
    rows, width = x.shape
    heads = bias.shape[0]
    hd = width // heads
    return pl.pallas_call(
        halo_kernel,
        out_shape=jax.ShapeDtypeStruct((copies, 1, width), jnp.float32),
        in_specs=[SMEM, SMEM] + [VMEM] * 9,
        out_specs=VMEM,
        scratch_shapes=[
            pltpu.VMEM((heads, rows, hd), jnp.bfloat16),
            pltpu.VMEM((heads, rows, hd), jnp.bfloat16),
            pltpu.VMEM((rows, 128), jnp.int32),
            pltpu.VMEM((heads, rows, hd), jnp.float32),
            pltpu.VMEM((rows, width), jnp.bfloat16),
        ],
        compiler_params=pltpu.CompilerParams(vmem_limit_bytes=24 << 20),
        name="halo_part",
    )(meta, bias, halo, w, halo_ids, ids, x, gate, q, part, w_out)


def shifted(block, axis, distance):
    devices = range(lax.axis_size(axis))
    route = [(i - distance, i) for i in devices if i - distance in devices]
    return lax.ppermute(block, axis, route)


def local_pool(events, item_ids, lengths, w_proj, w_out, repeat_bias):
    x = events[0]
    start = lax.axis_index("hist") * x.shape[0]
    meta = jnp.stack([lengths[0], start]).astype(jnp.int32)
    halo = shifted(x, "hist", 1)
    halo_ids = shifted(item_ids, "hist", 1)
    gate, q, part = own_part(meta, repeat_bias, x, w_proj, item_ids)
    copies = lax.axis_size("hist")
    return halo_part(
        copies, meta, repeat_bias, halo, w_proj, halo_ids, item_ids, x, gate, q, part, w_out
    )


def vector_kernel(parts_ref, out_ref):
    pooled = parts_ref[0]
    for j in range(1, parts_ref.shape[0]):
        pooled = pooled + parts_ref[j]
    normed = pooled * lax.rsqrt(jnp.mean(pooled * pooled, axis=1, keepdims=True) + 1e-06)
    normed = normed.astype(jnp.bfloat16).astype(jnp.float32)
    for j in range(out_ref.shape[0]):
        out_ref[j] = normed


def as_row(column):
    users = column.shape[0]
    square = jnp.concatenate(
        [jnp.broadcast_to(column, (users, 128)), jnp.zeros((128 - users, 128), jnp.float32)], axis=0
    )
    return square.T[:1]


def logit_kernel(vecs_ref, slab_ref, logits_ref, lse_ref):
    vecs = jnp.concatenate([vecs_ref[j] for j in range(vecs_ref.shape[0])], axis=0).astype(jnp.bfloat16)
    logits = 4.0 * lax.dot_general(vecs, slab_ref[...], NT, preferred_element_type=jnp.float32)
    logits_ref[...] = logits
    top = jnp.max(logits, axis=1, keepdims=True)
    lse = top + jnp.log(jnp.sum(jnp.exp(logits - top), axis=1, keepdims=True))
    row = as_row(lse)
    for j in range(lse_ref.shape[0]):
        lse_ref[j] = row


def joined(parts_ref):
    parts = [parts_ref[j] for j in range(parts_ref.shape[0])]
    top = functools.reduce(jnp.maximum, parts)
    return top + jnp.log(sum(jnp.exp(p - top) for p in parts))


def join_kernel(parts_ref, out_ref):
    lse = joined(parts_ref)
    for j in range(out_ref.shape[0]):
        out_ref[j] = lse


def final_kernel(parts_ref, logits_ref, out_ref):
    users = logits_ref.shape[0]
    lse = jnp.broadcast_to(joined(parts_ref), (128, 128)).T[:users, :1]
    out_ref[...] = logits_ref[...] - lse


def small(kernel, outs, *args, name):
    return pl.pallas_call(
        kernel,
        out_shape=outs,
        in_specs=[VMEM] * len(args),
        out_specs=jax.tree.map(lambda _: VMEM, outs),
        compiler_params=pltpu.CompilerParams(vmem_limit_bytes=16 << 20),
        name=name,
    )(*args)


def swapped(x, axis):
    return lax.all_to_all(x, axis, 0, 0, tiled=True)


def local(events, item_ids, lengths, w_proj, w_out, repeat_bias, item_slab):
    f32 = functools.partial(jax.ShapeDtypeStruct, dtype=jnp.float32)
    hists, items = lax.axis_size("hist"), lax.axis_size("item")
    users, width = items * events.shape[0], events.shape[2]
    parts = local_pool(events, item_ids, lengths, w_proj, w_out, repeat_bias)
    vecs = small(vector_kernel, f32((items, 1, width)), swapped(parts, "hist"), name="vectors")
    logits, lse = small(
        logit_kernel, (f32((users, item_slab.shape[0])), f32((hists, 1, 128))),
        swapped(vecs, "item"), item_slab, name="logits",
    )
    lse = small(join_kernel, f32((items, 1, 128)), swapped(lse, "hist"), name="join")
    return small(final_kernel, f32(logits.shape), swapped(lse, "item"), logits, name="final")


def solution(mesh):
    placed = (
        P("item", "hist", None),
        P("item", "hist"),
        P("item"),
        P(),
        P(),
        P(),
        P(("hist", "item"), None),
    )
    return jax.shard_map(
        local, mesh=mesh, in_specs=placed, out_specs=P(None, ("hist", "item")), check_vma=False
    )
```

time: 430 us -> 101 us (0.23)
  blocking collectives: 299 us -> 68.3 us
  local copies, waits for them, and re-layouts: 40.7 us -> 4.17 us
  matrix products: 31.8 us -> 0 us
  waiting for transfers between devices: 21.3 us -> 0.01 us
  Pallas kernels: 0 us -> 18.9 us
  other arithmetic: 18.8 us -> 0.08 us
  loops' own time: 7.86 us -> 0 us
    psum x2 -> x0, blocking collectives: 134 us -> none  [the longest x1 100 us: local(): lax.psum(jnp.sum(jnp.exp(logits - top_logit[:, None]), axis=1), ('hist',...]
    pmax x1 -> x0, blocking collectives: 111 us -> none  [local(): top_logit = lax.pmax(jnp.max(logits, axis=1), ('hist', 'item'))]
    all_to_all x0 -> x4, blocking collectives: none -> 68.3 us  [swapped(): return lax.all_to_all(x, axis, 0, 0, tiled=True)]
    all_gather x1 -> x0, blocking collectives: 54.2 us -> none  [local(): user_vecs = lax.all_gather(row_normed(pooled), 'item', axis=0, tiled=True)]
    dynamic_slice x36 -> x0, local copies, waits for them, and re-layouts: 35.3 us -> none  [the longest x32 32.9 us: take_rows(): return lax.dynamic_slice(array, starts, sizes)[0]]
    dot_general x10 -> x0, matrix products: 31.8 us -> none  [the longest x4 20.1 us: one_block(): jnp.einsum('hqk,khd->qhd', weights, value_rows, preferred_element_type=jn...]
    ppermute x2, waiting for transfers between devices: 21.3 us -> 0.01 us  [shifted(): return lax.ppermute(block, axis, route)]
    pallas_call x0 -> x6, Pallas kernels: none -> 18.9 us  [the longest x1 9.29 us: own_part(): pl.pallas_call(own_kernel, out_shape=(jax.ShapeDtypeStruct((rows, width),...]
  transfers between devices with their start and end apart: 2 -> 2, of which waited for: 1 -> 0; matrix products, arithmetic and copies ran while one was open for 0% -> 0% of each run, Pallas kernels for 0% -> 9%
where the time goes in v1:
time: 101 us; the launch traced here: 100 us
  blocking collectives  68.3 us (68%)
  Pallas kernels  18.9 us (19%)
  starting transfers between devices  7.94 us (8%)
  local copies, waits for them, and re-layouts  4.17 us (4%)
    all_to_all x4, blocking collectives, swapped(): return lax.all_to_all(x, axis, 0, 0, tiled=True)  68.3 us
    pallas_call x1, Pallas kernels, own_part(): pl.pallas_call(own_kernel, out_shape=(jax.ShapeDtypeStruct((rows, width),...  9.29 us
    ppermute x2, starting transfers between devices, shifted(): return lax.ppermute(block, axis, route)  7.94 us
    pallas_call x1, Pallas kernels, halo_part(): pl.pallas_call(halo_kernel, out_shape=jax.ShapeDtypeStruct((copies, 1, wi...  7.93 us
    unnamed x12, local copies, waits for them, and re-layouts  4.17 us
  transfers between devices with their start and end apart: 2, of which 0 were waited for; matrix products, arithmetic and copies ran while one was open for 0% of the time, Pallas kernels for 9%

profile of v1, /device:TPU:1, one launch (start us, length us, event | category | flops | bytes accessed | tf_op | source)
XLA Modules:
  0.0 100.2 jit_solution(7568725164087705446)
XLA Ops:
  0.0 6.0 %collective-permute-start = (bf16[1024,512]{1,0:T(8,128)(2,1)}, bf16[1024,512]{1,0:T(8,128)(2,1)S(1)}, u32[]{:S(2)}, u32[]{:S(2)}) collective-permute-start(bf16[1024,512]{1,0:T(8,128)(2,1)} %bitcast.2), channel_id=1, source_target_pairs={{0,32},{32,64},{64,96},{96,128},{128,160},{160,192},{192,224},{224... | collective-permute-start | bytes 3145736 | tf_op jit(solution)/shard_map/ppermute | solution.py:199
  6.0 1.9 %collective-permute-start.1 = (s32[1,1024]{1,0:T(1,128)}, s32[1,1024]{1,0:T(1,128)S(1)}, u32[]{:S(2)}, u32[]{:S(2)}) collective-permute-start(s32[1,1024]{1,0:T(1,128)} %own_ids_ref.1), channel_id=1, source_target_pairs={{0,32},{32,64},{64,96},{96,128},{128,160},{160,192},{192,224},{224... | collective-permute-start | bytes 12296 | tf_op jit(solution)/shard_map/ppermute | solution.py:199
  8.6 0.1 pad_add_fusion.meta
  8.7 0.0 copy-start
  8.7 1.6 %copy-done = bf16[512,2048]{1,0:T(8,128)(2,1)S(1)} copy-done((bf16[512,2048]{1,0:T(8,128)(2,1)S(1)}, bf16[512,2048]{1,0:T(8,128)(2,1)}, u32[]{:S(2)}) %copy-start) | copy-done | bytes 2097176
  10.3 0.0 copy-start.2
  10.3 1.2 %copy-done.2 = bf16[1,1024,512]{2,1,0:T(8,128)(2,1)S(1)} copy-done((bf16[1,1024,512]{2,1,0:T(8,128)(2,1)S(1)}, bf16[1,1024,512]{2,1,0:T(8,128)(2,1)}, u32[]{:S(2)}) %copy-start.2) | copy-done | bytes 1048600
  11.5 0.0 copy-start.4
  11.5 0.7 copy-done.4
  12.2 0.0 copy-start.5
  12.2 0.7 copy-done.5
  12.8 0.0 copy-start.3
  12.8 9.3 %own_part.1 = (bf16[1024,512]{1,0:T(8,128)(2,1)S(1)}, bf16[4,1024,128]{2,1,0:T(8,128)(2,1)S(1)}, f32[4,1024,128]{2,1,0:T(8,128)S(1)}) custom-call(s32[2]{0:T(128)S(1)} %pad_add_fusion.meta, f32[4]{0:T(128)S(1)} %copy-done.5, bf16[1024,512]{1,0:T(8,128)(2,1)S(1)} %bitcast.3, bf16[512,2048]{1,0:T(8,128)(2,1)S(1)} %copy-done, s32[1,1024]{1,0:T(1,128)S(1)} %copy-done.4), custom_call_target="tpu_custom_call" | custom-call | flops 8000000000 | bytes 10000000 | tf_op jit(solution)/shard_map/own_part/pallas_call | solution.py:155
  22.1 0.0 collective-permute-done.1.ids_ref
  22.2 0.0 collective-permute-done.x_ref
  22.2 0.0 copy-done.3
  22.2 0.0 copy-start.1
  22.2 7.9 %halo_part.1 = f32[16,1,512]{2,1,0:T(1,128)S(1)} custom-call(s32[2]{0:T(128)S(1)} %pad_add_fusion.meta, f32[4]{0:T(128)S(1)} %copy-done.5, bf16[1024,512]{1,0:T(8,128)(2,1)S(1)} %collective-permute-done.x_ref, bf16[512,2048]{1,0:T(8,128)(2,1)S(1)} %copy-done, s32[1,1024]{1,0:T(1,128)S(1)} %collective-permute-done.1.ids_ref, s32[1,1024]{1,0:T(1,128)S(1)} %copy-done.4, ...), custom_call_target="tpu_custom_call" | custom-call | tf_op jit(solution)/shard_map/halo_part/pallas_call | solution.py:179
  30.1 12.7 %all_to_all.20.parts_ref = f32[16,1,512]{2,1,0:T(1,128)S(1)} all-to-all(f32[16,1,512]{2,1,0:T(1,128)S(1)} %halo_part.1), channel_id=1, replica_groups=mesh['hist'=16,'item'=32] {'hist'}, dimensions={0} | all-to-all | bytes 65536 | tf_op jit(solution)/shard_map/all_to_all | solution.py:274
  42.9 0.1 vectors.1
  43.0 28.5 %all_to_all.21.vecs_ref = f32[32,1,512]{2,1,0:T(1,128)S(1)} all-to-all(f32[32,1,512]{2,1,0:T(1,128)S(1)} %vectors.1), channel_id=1, replica_groups=mesh['hist'=16,'item'=32] {'item'}, dimensions={0} | all-to-all | bytes 131072 | tf_op jit(solution)/shard_map/all_to_all | solution.py:274
  71.5 0.0 copy-done.1
  71.5 0.7 logits.1
  72.2 12.0 %all_to_all.22.parts_ref = f32[16,1,128]{2,1,0:T(1,128)S(1)} all-to-all(f32[16,1,128]{2,1,0:T(1,128)S(1)} %get-tuple-element.13), channel_id=1, replica_groups=mesh['hist'=16,'item'=32] {'hist'}, dimensions={0} | all-to-all | bytes 16384 | tf_op jit(solution)/shard_map/all_to_all | solution.py:274
  84.2 0.1 join.1
  84.2 15.1 %all_to_all.23.parts_ref = f32[32,1,128]{2,1,0:T(1,128)S(1)} all-to-all(f32[32,1,128]{2,1,0:T(1,128)S(1)} %join.1), channel_id=1, replica_groups=mesh['hist'=16,'item'=32] {'item'}, dimensions={0} | all-to-all | bytes 32768 | tf_op jit(solution)/shard_map/all_to_all | solution.py:274
  99.3 0.9 final.1
Async XLA Ops:
  0.0 22.2 %collective-permute-start = (bf16[1024,512]{1,0:T(8,128)(2,1)}, bf16[1024,512]{1,0:T(8,128)(2,1)S(1)}, u32[]{:S(2)}, u32[]{:S(2)}) collective-permute-start(bf16[1024,512]{1,0:T(8,128)(2,1)} %bitcast.2), channel_id=1, source_target_pairs={{0,32},{32,64},{64,96},{96,128},{128,160},{160,192},{192,224},{224... | collective-permute-start | bytes 3145736 | tf_op jit(solution)/shard_map/ppermute | solution.py:199
  6.0 16.1 %collective-permute-start.1 = (s32[1,1024]{1,0:T(1,128)}, s32[1,1024]{1,0:T(1,128)S(1)}, u32[]{:S(2)}, u32[]{:S(2)}) collective-permute-start(s32[1,1024]{1,0:T(1,128)} %own_ids_ref.1), channel_id=1, source_target_pairs={{0,32},{32,64},{64,96},{96,128},{128,160},{160,192},{192,224},{224... | collective-permute-start | bytes 12296 | tf_op jit(solution)/shard_map/ppermute | solution.py:199
  8.7 1.6 %copy-start = (bf16[512,2048]{1,0:T(8,128)(2,1)S(1)}, bf16[512,2048]{1,0:T(8,128)(2,1)}, u32[]{:S(2)}) copy-start(bf16[512,2048]{1,0:T(8,128)(2,1)} %w_ref.3) | copy-start | bytes 6291460
  10.3 1.2 %copy-start.2 = (bf16[1,1024,512]{2,1,0:T(8,128)(2,1)S(1)}, bf16[1,1024,512]{2,1,0:T(8,128)(2,1)}, u32[]{:S(2)}) copy-start(bf16[1,1024,512]{2,1,0:T(8,128)(2,1)} %param.7) | copy-start | bytes 3145732
  11.5 0.7 copy-start.4
  12.2 0.7 copy-start.5
  12.8 9.3 %copy-start.3 = (bf16[512,512]{1,0:T(8,128)(2,1)S(1)}, bf16[512,512]{1,0:T(8,128)(2,1)}, u32[]{:S(2)}) copy-start(bf16[512,512]{1,0:T(8,128)(2,1)} %w_out_ref.1) | copy-start | bytes 1572868
  22.2 49.3 %copy-start.1 = (bf16[1024,512]{1,0:T(8,128)(2,1)S(1)}, bf16[1024,512]{1,0:T(8,128)(2,1)}, u32[]{:S(2)}) copy-start(bf16[1024,512]{1,0:T(8,128)(2,1)} %slab_ref.1) | copy-start | bytes 3145732

commit v2 on v1

v2 whole, which is shorter than its diff:
```python
import functools
import math

import jax
import jax.numpy as jnp
from jax import lax
from jax.experimental import pallas as pl
from jax.experimental.pallas import tpu as pltpu
from jax.sharding import PartitionSpec as P

WINDOW = 1024
BLOCK = 256
NT = (((1,), (1,)), ((), ()))


def mm(a, b):
    return jnp.dot(a, b, preferred_element_type=jnp.float32)


def silu(x):
    half = 0.5 * x
    return half * jnp.tanh(half) + half


def spread_ids(ids_ref, out_ref):
    for b in range(out_ref.shape[0] // 128):
        row = ids_ref[:, b * 128 : (b + 1) * 128]
        out_ref[b * 128 : (b + 1) * 128, :] = jnp.broadcast_to(row, (128, 128)).T


def weigh(half, qid, kid, bias, keep):
    same = jnp.concatenate([qid] * (half.shape[1] // 128), axis=1) == kid
    half = half + jnp.where(same, bias, 0.0)
    weights = half * jnp.tanh(half) + half
    if keep is not None:
        weights = jnp.where(keep, weights, 0.0)
    return weights.astype(jnp.bfloat16)


def attend(pairs, q_of, k_of, v_of, qid_of, kid_of, bias, keep_of, start_of, store):
    steps = [(r, c) for r, cs in pairs for c in cs]

    def scores(step):
        return lax.dot_general(q_of(step[0]), k_of(step[1]), NT, preferred_element_type=jnp.float32)

    ahead = scores(steps[0])
    done = 0
    for r, cs in pairs:
        acc = start_of(r)
        for c in cs:
            half = ahead
            done += 1
            if done < len(steps):
                ahead = scores(steps[done])
            weights = weigh(half, qid_of(r), kid_of(c), bias, keep_of(r, c))
            term = mm(weights, v_of(c))
            acc = term if acc is None else acc + term
        store(r, acc)


def triangle():
    row = lax.broadcasted_iota(jnp.int32, (BLOCK, BLOCK), 0)
    col = lax.broadcasted_iota(jnp.int32, (BLOCK, BLOCK), 1)
    return col <= row


def part(b):
    return slice(b * BLOCK, (b + 1) * BLOCK)


def own_kernel(
    x_hbm, w_hbm, ids_hbm, bias_hbm, length_ref, gate_ref, q_ref, part_ref,
    x_ref, w_ref, ids_ref, bias_ref, k_buf, v_buf, qid_buf, sems, w_sems,
):
    rows, width = x_ref.shape
    heads = q_ref.shape[0]
    hd = width // heads
    blocks = rows // BLOCK
    cols = w_sems.shape[0]
    start = lax.axis_index("hist") * rows
    fetches = [
        pltpu.make_async_copy(x_hbm.at[0], x_ref, sems.at[0]),
        pltpu.make_async_copy(ids_hbm, ids_ref, sems.at[1]),
        pltpu.make_async_copy(bias_hbm, bias_ref, sems.at[2]),
    ]
    step = w_hbm.shape[1] // cols
    w_fetches = [
        pltpu.make_async_copy(
            w_hbm.at[:, c * step : (c + 1) * step], w_ref.at[:, c * step : (c + 1) * step], w_sems.at[c]
        )
        for c in range(cols)
    ]
    for copy in fetches[:1] + w_fetches + fetches[1:]:
        copy.start()
    fetches[0].wait()
    scale = 0.5 / math.sqrt(hd)
    for c in range(cols):
        w_fetches[c].wait()
        at = c * step
        kind, at = at // width, at % width
        for r in range(0, rows, M):
            rs = slice(r, r + M)
            y = silu(mm(x_ref[rs, :], w_ref[:, c * step : (c + 1) * step]))
            if kind == 0:
                gate_ref[rs, at : at + step] = y
                continue
            if kind == 1:
                pos = start + r + lax.broadcasted_iota(jnp.int32, (M, 1), 0)
                y = jnp.where(pos < length_ref[0], y, 0.0)
            if kind == 2:
                y = y.astype(jnp.bfloat16).astype(jnp.float32) * scale
            y = y.astype(jnp.bfloat16)
            buf = (None, v_buf, q_ref, k_buf)[kind]
            for h in range(step // hd):
                buf[at // hd + h, rs, :] = y[:, h * hd : (h + 1) * hd]
    for copy in fetches[1:]:
        copy.wait()
    spread_ids(ids_ref, qid_buf)
    keep = triangle()

    def head(h, carry):
        def store(r, acc):
            part_ref[h, part(r), :] = acc

        attend(
            [(r, range(r + 1)) for r in range(blocks)],
            lambda r: q_ref[h, part(r), :], lambda c: k_buf[h, part(c), :], lambda c: v_buf[h, part(c), :],
            lambda r: qid_buf[part(r), :], lambda c: ids_ref[:, part(c)], 0.5 * bias_ref[h],
            lambda r, c: keep if r == c else None, lambda r: None, store,
        )
        return carry

    lax.fori_loop(0, heads, head, 0)


def halo_kernel(
    length_ref, bias_ref, x_ref, w_ref, ids_ref, own_ids_ref, events_ref, gate_ref, q_ref, part_ref, w_out_ref,
    out_ref, k_buf, v_buf, qid_buf, mix_buf, gated_buf,
):
    rows, width = x_ref.shape
    heads = q_ref.shape[0]
    hd = width // heads
    blocks = rows // BLOCK
    length, start = length_ref[0], lax.axis_index("hist") * rows
    spread_ids(own_ids_ref, qid_buf)
    step = 256
    for kind, buf in ((1, v_buf), (3, k_buf)):
        for at in range(0, width, step):
            for r in range(0, rows, M):
                rs = slice(r, r + M)
                y = silu(mm(x_ref[rs, :], w_ref[:, kind * width + at : kind * width + at + step]))
                if kind == 1:
                    pos = start - WINDOW + r + lax.broadcasted_iota(jnp.int32, (M, 1), 0)
                    y = jnp.where((pos >= 0) & (pos < length), y, 0.0)
                y = y.astype(jnp.bfloat16)
                for h in range(step // hd):
                    buf[at // hd + h, rs, :] = y[:, h * hd : (h + 1) * hd]
    keep = jnp.logical_not(triangle())

    def head(h, carry):
        def store(r, acc):
            mix_buf[h, part(r), :] = acc

        attend(
            [(r, range(r, blocks)) for r in range(blocks)],
            lambda r: q_ref[h, part(r), :], lambda c: k_buf[h, part(c), :], lambda c: v_buf[h, part(c), :],
            lambda r: qid_buf[part(r), :], lambda c: ids_ref[:, part(c)], 0.5 * bias_ref[h],
            lambda r, c: keep if r == c else None, lambda r: part_ref[h, part(r), :], store,
        )
        return carry

    lax.fori_loop(0, heads, head, 0)

    def norm_rows(b, carry):
        rs = pl.ds(pl.multiple_of(b * NORM_ROWS, NORM_ROWS), NORM_ROWS)
        mixed = [mix_buf[h, rs, :] for h in range(heads)]
        mean = jnp.sum(sum(mixed), axis=1, keepdims=True) * (1.0 / width)
        mixed = [m - mean for m in mixed]
        spread = jnp.sum(sum(m * m for m in mixed), axis=1, keepdims=True) * (1.0 / width)
        factor = lax.rsqrt(spread + 1e-06 * WINDOW * WINDOW)
        for h in range(heads):
            gated = mixed[h] * factor * gate_ref[rs, h * hd : (h + 1) * hd]
            gated_buf[rs, h * hd : (h + 1) * hd] = gated.astype(jnp.bfloat16)
        return carry

    lax.fori_loop(0, rows // NORM_ROWS, norm_rows, 0, unroll=NORM_UNROLL)
    place = start + lax.broadcasted_iota(jnp.int32, (8, rows), 1)
    counted = jnp.where(place < length, 1.0, 0.0).astype(jnp.bfloat16)
    gated_sum = mm(counted, gated_buf[...])
    event_sum = mm(counted, events_ref[...])
    projected = jnp.dot(
        gated_sum, w_out_ref[...].astype(jnp.float32),
        preferred_element_type=jnp.float32, precision=lax.Precision.HIGHEST,
    )
    total = (projected + event_sum)[:1]
    for j in range(out_ref.shape[0]):
        out_ref[j] = total


M = 512
NORM_ROWS = 32
NORM_UNROLL = 4
SMEM = pl.BlockSpec(memory_space=pltpu.SMEM)
VMEM = pl.BlockSpec(memory_space=pltpu.VMEM)


HBM = pl.BlockSpec(memory_space=pltpu.MemorySpace.HBM)


def own_part(events, w, ids, length, bias):
    _, rows, width = events.shape
    heads = bias.shape[0]
    hd = width // heads
    cols = 4
    return pl.pallas_call(
        own_kernel,
        out_shape=(
            jax.ShapeDtypeStruct((rows, width), jnp.float32),
            jax.ShapeDtypeStruct((heads, rows, hd), jnp.bfloat16),
            jax.ShapeDtypeStruct((heads, rows, hd), jnp.float32),
        ),
        in_specs=[HBM] * 4 + [SMEM],
        out_specs=(VMEM, VMEM, VMEM),
        scratch_shapes=[
            pltpu.VMEM((rows, width), jnp.bfloat16),
            pltpu.VMEM(w.shape, jnp.bfloat16),
            pltpu.VMEM(ids.shape, jnp.int32),
            pltpu.SMEM(bias.shape, jnp.float32),
            pltpu.VMEM((heads, rows, hd), jnp.bfloat16),
            pltpu.VMEM((heads, rows, hd), jnp.bfloat16),
            pltpu.VMEM((rows, 128), jnp.int32),
            pltpu.SemaphoreType.DMA((3,)),
            pltpu.SemaphoreType.DMA((cols,)),
        ],
        compiler_params=pltpu.CompilerParams(vmem_limit_bytes=26 << 20),
        cost_estimate=pl.CostEstimate(flops=8 * 10**9, bytes_accessed=10**7, transcendentals=4 * 10**6),
        name="own_part",
    )(*[pltpu.with_memory_space_constraint(a, pltpu.MemorySpace.HBM) for a in (events, w, ids, bias)], length)


def halo_part(copies, length, bias, halo, w, halo_ids, ids, x, gate, q, part, w_out):
    rows, width = x.shape
    heads = bias.shape[0]
    hd = width // heads
    return pl.pallas_call(
        halo_kernel,
        out_shape=jax.ShapeDtypeStruct((copies, 1, width), jnp.float32),
        in_specs=[SMEM, SMEM] + [VMEM] * 9,
        out_specs=VMEM,
        scratch_shapes=[
            pltpu.VMEM((heads, rows, hd), jnp.bfloat16),
            pltpu.VMEM((heads, rows, hd), jnp.bfloat16),
            pltpu.VMEM((rows, 128), jnp.int32),
            pltpu.VMEM((heads, rows, hd), jnp.float32),
            pltpu.VMEM((rows, width), jnp.bfloat16),
        ],
        compiler_params=pltpu.CompilerParams(vmem_limit_bytes=24 << 20),
        name="halo_part",
    )(length, bias, halo, w, halo_ids, ids, x, gate, q, part, w_out)


def shifted(block, axis, distance):
    devices = range(lax.axis_size(axis))
    route = [(i - distance, i) for i in devices if i - distance in devices]
    return lax.ppermute(block, axis, route)


def local_pool(events, item_ids, lengths, w_proj, w_out, repeat_bias):
    x = events[0]
    halo = shifted(x, "hist", 1)
    halo_ids = shifted(item_ids, "hist", 1)
    gate, q, part = own_part(events, w_proj, item_ids, lengths, repeat_bias)
    copies = lax.axis_size("hist")
    return halo_part(
        copies, lengths, repeat_bias, halo, w_proj, halo_ids, item_ids, x, gate, q, part, w_out
    )


def vector_kernel(parts_ref, out_ref):
    pooled = parts_ref[0]
    for j in range(1, parts_ref.shape[0]):
        pooled = pooled + parts_ref[j]
    normed = pooled * lax.rsqrt(jnp.mean(pooled * pooled, axis=1, keepdims=True) + 1e-06)
    normed = normed.astype(jnp.bfloat16).astype(jnp.float32)
    for j in range(out_ref.shape[0]):
        out_ref[j] = normed


def as_row(column):
    users = column.shape[0]
    square = jnp.concatenate(
        [jnp.broadcast_to(column, (users, 128)), jnp.zeros((128 - users, 128), jnp.float32)], axis=0
    )
    return square.T[:1]


def logit_kernel(vecs_ref, slab_ref, logits_ref, lse_ref):
    vecs = jnp.concatenate([vecs_ref[j] for j in range(vecs_ref.shape[0])], axis=0).astype(jnp.bfloat16)
    logits = 4.0 * lax.dot_general(vecs, slab_ref[...], NT, preferred_element_type=jnp.float32)
    logits_ref[...] = logits
    top = jnp.max(logits, axis=1, keepdims=True)
    lse = top + jnp.log(jnp.sum(jnp.exp(logits - top), axis=1, keepdims=True))
    row = as_row(lse)
    for j in range(lse_ref.shape[0]):
        lse_ref[j] = row


def joined(parts_ref):
    parts = [parts_ref[j] for j in range(parts_ref.shape[0])]
    top = functools.reduce(jnp.maximum, parts)
    return top + jnp.log(sum(jnp.exp(p - top) for p in parts))


def join_kernel(parts_ref, out_ref):
    lse = joined(parts_ref)
    for j in range(out_ref.shape[0]):
        out_ref[j] = lse


def final_kernel(parts_ref, logits_ref, out_ref):
    users = logits_ref.shape[0]
    lse = jnp.broadcast_to(joined(parts_ref), (128, 128)).T[:users, :1]
    out_ref[...] = logits_ref[...] - lse


def small(kernel, outs, *args, name):
    return pl.pallas_call(
        kernel,
        out_shape=outs,
        in_specs=[VMEM] * len(args),
        out_specs=jax.tree.map(lambda _: VMEM, outs),
        compiler_params=pltpu.CompilerParams(vmem_limit_bytes=16 << 20),
        name=name,
    )(*args)


def swapped(x, axis):
    return lax.all_to_all(x, axis, 0, 0, tiled=True)


def local(events, item_ids, lengths, w_proj, w_out, repeat_bias, item_slab):
    f32 = functools.partial(jax.ShapeDtypeStruct, dtype=jnp.float32)
    hists, items = lax.axis_size("hist"), lax.axis_size("item")
    users, width = items * events.shape[0], events.shape[2]
    parts = local_pool(events, item_ids, lengths, w_proj, w_out, repeat_bias)
    vecs = small(vector_kernel, f32((items, 1, width)), swapped(parts, "hist"), name="vectors")
    logits, lse = small(
        logit_kernel, (f32((users, item_slab.shape[0])), f32((hists, 1, 128))),
        swapped(vecs, "item"), item_slab, name="logits",
    )
    lse = small(join_kernel, f32((items, 1, 128)), swapped(lse, "hist"), name="join")
    return small(final_kernel, f32(logits.shape), swapped(lse, "item"), logits, name="final")


def solution(mesh):
    placed = (
        P("item", "hist", None),
        P("item", "hist"),
        P("item"),
        P(),
        P(),
        P(),
        P(("hist", "item"), None),
    )
    return jax.shard_map(
        local, mesh=mesh, in_specs=placed, out_specs=P(None, ("hist", "item")), check_vma=False
    )
```

time: 101 us -> 99.3 us (0.983)
  local copies, waits for them, and re-layouts: 4.17 us -> 0.03 us
  Pallas kernels: 18.9 us -> 21.9 us
    unnamed x12, local copies, waits for them, and re-layouts: 4.17 us -> 0.03 us
    pallas_call x1, Pallas kernels: 9.29 us -> 11.1 us  [own_part(): pl.pallas_call(own_kernel, out_shape=(jax.ShapeDtypeStruct((rows, width),...]
    pallas_call x1, Pallas kernels: 7.93 us -> 9.12 us  [halo_part(): pl.pallas_call(halo_kernel, out_shape=jax.ShapeDtypeStruct((copies, 1, wi...]
  transfers between devices with their start and end apart: 2 -> 2, of which waited for: 0 -> 0; matrix products, arithmetic and copies ran while one was open for 0% -> 0% of each run, Pallas kernels for 9% -> 11%
where the time goes in v2:
time: 99.3 us; the launch traced here: 99 us
  blocking collectives  68.3 us (69%)
  Pallas kernels  21.9 us (22%)
  starting transfers between devices  7.94 us (8%)
    all_to_all x4, blocking collectives, swapped(): return lax.all_to_all(x, axis, 0, 0, tiled=True)  68.3 us
    pallas_call x1, Pallas kernels, own_part(): pl.pallas_call(own_kernel, out_shape=(jax.ShapeDtypeStruct((rows, width),...  11.1 us
    pallas_call x1, Pallas kernels, halo_part(): pl.pallas_call(halo_kernel, out_shape=jax.ShapeDtypeStruct((copies, 1, wi...  9.12 us
    ppermute x2, starting transfers between devices, shifted(): return lax.ppermute(block, axis, route)  7.94 us
  transfers between devices with their start and end apart: 2, of which 0 were waited for; matrix products, arithmetic and copies ran while one was open for 0% of the time, Pallas kernels for 11%

profile of v2, /device:TPU:1, one launch (start us, length us, event | category | flops | bytes accessed | tf_op | source)
XLA Modules:
  0.0 99.0 jit_solution(13543654077872882650)
XLA Ops:
  0.0 6.0 %collective-permute-start = (bf16[1024,512]{1,0:T(8,128)(2,1)}, bf16[1024,512]{1,0:T(8,128)(2,1)S(1)}, u32[]{:S(2)}, u32[]{:S(2)}) collective-permute-start(bf16[1024,512]{1,0:T(8,128)(2,1)} %bitcast.1), channel_id=1, source_target_pairs={{0,32},{32,64},{64,96},{96,128},{128,160},{160,192},{192,224},{224... | collective-permute-start | bytes 3145736 | tf_op jit(solution)/shard_map/ppermute | solution.py:265
  6.0 1.9 %collective-permute-start.1 = (s32[1,1024]{1,0:T(1,128)}, s32[1,1024]{1,0:T(1,128)S(1)}, u32[]{:S(2)}, u32[]{:S(2)}) collective-permute-start(s32[1,1024]{1,0:T(1,128)} %own_ids_ref.1), channel_id=1, source_target_pairs={{0,32},{32,64},{64,96},{96,128},{128,160},{160,192},{192,224},{224... | collective-permute-start | bytes 12296 | tf_op jit(solution)/shard_map/ppermute | solution.py:265
  8.6 0.0 copy-start
  8.6 0.0 copy-start.1
  8.6 0.0 copy-start.3
  8.6 0.0 copy-start.4
  8.6 0.0 copy-start.5
  8.6 11.1 %own_part.1 = (f32[1024,512]{1,0:T(8,128)S(1)}, bf16[4,1024,128]{2,1,0:T(8,128)(2,1)S(1)}, f32[4,1024,128]{2,1,0:T(8,128)S(1)}) custom-call(bf16[1,1024,512]{2,1,0:T(8,128)(2,1)} %x_hbm.1, bf16[512,2048]{1,0:T(8,128)(2,1)} %w_ref.1, s32[1,1024]{1,0:T(1,128)} %own_ids_ref.1, f32[4]{0:T(128)} %bias_ref.1, s32[1]{0:T(128)S(6)} %copy.8.length_ref), custom_call_target="tpu_custom_call" | custom-call | flops 8000000000 | bytes 10000000 | tf_op jit(solution)/shard_map/own_part/pallas_call | solution.py:215
  19.7 0.0 collective-permute-done.1.ids_ref
  19.7 0.0 collective-permute-done.x_ref
  19.7 0.0 copy-done
  19.8 0.0 copy-done.1
  19.8 0.0 copy-done.3
  19.8 0.0 copy-done.4
  19.8 0.0 copy-done.5
  19.8 0.0 copy-start.2
  19.8 9.1 %halo_part.1 = f32[16,1,512]{2,1,0:T(1,128)S(1)} custom-call(s32[1]{0:T(128)S(6)} %copy.8.length_ref, f32[4]{0:T(128)S(1)} %copy-done.5, bf16[1024,512]{1,0:T(8,128)(2,1)S(1)} %collective-permute-done.x_ref, bf16[512,2048]{1,0:T(8,128)(2,1)S(1)} %copy-done, s32[1,1024]{1,0:T(1,128)S(1)} %collective-permute-done.1.ids_ref, s32[1,1024]{1,0:T(1,128)S(1)} %copy-done.4, ...), custom_call_target="tpu_custom_call" | custom-call | tf_op jit(solution)/shard_map/halo_part/pallas_call | solution.py:245
  28.9 13.7 %all_to_all.20.parts_ref = f32[16,1,512]{2,1,0:T(1,128)S(1)} all-to-all(f32[16,1,512]{2,1,0:T(1,128)S(1)} %halo_part.1), channel_id=1, replica_groups=mesh['hist'=16,'item'=32] {'hist'}, dimensions={0} | all-to-all | bytes 65536 | tf_op jit(solution)/shard_map/all_to_all | solution.py:338
  42.6 0.1 vectors.1
  42.7 27.6 %all_to_all.21.vecs_ref = f32[32,1,512]{2,1,0:T(1,128)S(1)} all-to-all(f32[32,1,512]{2,1,0:T(1,128)S(1)} %vectors.1), channel_id=1, replica_groups=mesh['hist'=16,'item'=32] {'item'}, dimensions={0} | all-to-all | bytes 131072 | tf_op jit(solution)/shard_map/all_to_all | solution.py:338
  70.3 0.0 copy-done.2
  70.3 0.7 logits.1
  71.0 12.0 %all_to_all.22.parts_ref = f32[16,1,128]{2,1,0:T(1,128)S(1)} all-to-all(f32[16,1,128]{2,1,0:T(1,128)S(1)} %get-tuple-element.13), channel_id=1, replica_groups=mesh['hist'=16,'item'=32] {'hist'}, dimensions={0} | all-to-all | bytes 16384 | tf_op jit(solution)/shard_map/all_to_all | solution.py:338
  83.0 0.1 join.1
  83.0 15.1 %all_to_all.23.parts_ref = f32[32,1,128]{2,1,0:T(1,128)S(1)} all-to-all(f32[32,1,128]{2,1,0:T(1,128)S(1)} %join.1), channel_id=1, replica_groups=mesh['hist'=16,'item'=32] {'item'}, dimensions={0} | all-to-all | bytes 32768 | tf_op jit(solution)/shard_map/all_to_all | solution.py:338
  98.1 0.9 final.1
Async XLA Ops:
  0.0 19.7 %collective-permute-start = (bf16[1024,512]{1,0:T(8,128)(2,1)}, bf16[1024,512]{1,0:T(8,128)(2,1)S(1)}, u32[]{:S(2)}, u32[]{:S(2)}) collective-permute-start(bf16[1024,512]{1,0:T(8,128)(2,1)} %bitcast.1), channel_id=1, source_target_pairs={{0,32},{32,64},{64,96},{96,128},{128,160},{160,192},{192,224},{224... | collective-permute-start | bytes 3145736 | tf_op jit(solution)/shard_map/ppermute | solution.py:265
  6.0 13.7 %collective-permute-start.1 = (s32[1,1024]{1,0:T(1,128)}, s32[1,1024]{1,0:T(1,128)S(1)}, u32[]{:S(2)}, u32[]{:S(2)}) collective-permute-start(s32[1,1024]{1,0:T(1,128)} %own_ids_ref.1), channel_id=1, source_target_pairs={{0,32},{32,64},{64,96},{96,128},{128,160},{160,192},{192,224},{224... | collective-permute-start | bytes 12296 | tf_op jit(solution)/shard_map/ppermute | solution.py:265
  8.6 11.1 %copy-start = (bf16[512,2048]{1,0:T(8,128)(2,1)S(1)}, bf16[512,2048]{1,0:T(8,128)(2,1)}, u32[]{:S(2)}) copy-start(bf16[512,2048]{1,0:T(8,128)(2,1)} %w_ref.1) | copy-start | bytes 6291460
  8.6 11.1 %copy-start.1 = (bf16[1,1024,512]{2,1,0:T(8,128)(2,1)S(1)}, bf16[1,1024,512]{2,1,0:T(8,128)(2,1)}, u32[]{:S(2)}) copy-start(bf16[1,1024,512]{2,1,0:T(8,128)(2,1)} %x_hbm.1) | copy-start | bytes 3145732
  8.6 11.1 %copy-start.3 = (bf16[512,512]{1,0:T(8,128)(2,1)S(1)}, bf16[512,512]{1,0:T(8,128)(2,1)}, u32[]{:S(2)}) copy-start(bf16[512,512]{1,0:T(8,128)(2,1)} %w_out_ref.1) | copy-start | bytes 1572868
  8.6 11.1 %copy-start.4 = (s32[1,1024]{1,0:T(1,128)S(1)}, s32[1,1024]{1,0:T(1,128)}, u32[]{:S(2)}) copy-start(s32[1,1024]{1,0:T(1,128)} %own_ids_ref.1) | copy-start | bytes 12292
  8.6 11.1 %copy-start.5 = (f32[4]{0:T(128)S(1)}, f32[4]{0:T(128)}, u32[]{:S(2)}) copy-start(f32[4]{0:T(128)} %bias_ref.1) | copy-start | bytes 52
  19.8 50.5 %copy-start.2 = (bf16[1024,512]{1,0:T(8,128)(2,1)S(1)}, bf16[1024,512]{1,0:T(8,128)(2,1)}, u32[]{:S(2)}) copy-start(bf16[1024,512]{1,0:T(8,128)(2,1)} %slab_ref.1) | copy-start | bytes 3145732

commit v3 on v2

--- a/solution.py
+++ b/solution.py
@@ -28,148 +28,130 @@
         out_ref[b * 128 : (b + 1) * 128, :] = jnp.broadcast_to(row, (128, 128)).T
 
 
-def weigh(half, qid, kid, bias, keep):
-    same = jnp.concatenate([qid] * (half.shape[1] // 128), axis=1) == kid
-    half = half + jnp.where(same, bias, 0.0)
-    weights = half * jnp.tanh(half) + half
-    if keep is not None:
-        weights = jnp.where(keep, weights, 0.0)
-    return weights.astype(jnp.bfloat16)
-
-
-def attend(pairs, q_of, k_of, v_of, qid_of, kid_of, bias, keep_of, start_of, store):
-    steps = [(r, c) for r, cs in pairs for c in cs]
-
-    def scores(step):
-        return lax.dot_general(q_of(step[0]), k_of(step[1]), NT, preferred_element_type=jnp.float32)
-
-    ahead = scores(steps[0])
-    done = 0
-    for r, cs in pairs:
-        acc = start_of(r)
-        for c in cs:
-            half = ahead
-            done += 1
-            if done < len(steps):
-                ahead = scores(steps[done])
-            weights = weigh(half, qid_of(r), kid_of(c), bias, keep_of(r, c))
-            term = mm(weights, v_of(c))
-            acc = term if acc is None else acc + term
-        store(r, acc)
-
-
-def triangle():
-    row = lax.broadcasted_iota(jnp.int32, (BLOCK, BLOCK), 0)
-    col = lax.broadcasted_iota(jnp.int32, (BLOCK, BLOCK), 1)
-    return col <= row
-
-
 def part(b):
     return slice(b * BLOCK, (b + 1) * BLOCK)
 
 
+def mark_same(row_ids_ref, col_ids_ref, spread, out_ref, row_blocks):
+    spread_ids(row_ids_ref, spread)
+    for c, rows in enumerate(row_blocks):
+        for r in rows:
+            mine = jnp.concatenate([spread[part(r), :]] * (BLOCK // 128), axis=1)
+            same = mine == col_ids_ref[:, part(c)]
+            out_ref[part(r), part(c)] = jnp.where(same, 1.0, 0.0)
+
+
+def weigh(half, same, bias):
+    half = half + same * bias
+    return (half * jnp.tanh(half) + half).astype(jnp.bfloat16)
+
+
+def columns(x_ref, w_ref, first, count, step, emit):
+    for at in range(first, first + count, step):
+        half = mm(x_ref[...], w_ref[:, at : at + step])
+        emit(at, half * jnp.tanh(half) + half)
+
+
+def put_heads(buf, at, y, hd):
+    y = y.astype(jnp.bfloat16)
+    for h in range(y.shape[1] // hd):
+        buf[at // hd + h] = y[:, h * hd : (h + 1) * hd]
+
+
 def own_kernel(
     x_hbm, w_hbm, ids_hbm, bias_hbm, length_ref, gate_ref, q_ref, part_ref,
-    x_ref, w_ref, ids_ref, bias_ref, k_buf, v_buf, qid_buf, sems, w_sems,
+    x_ref, w_ref, ids_ref, bias_ref, k_buf, v_buf, spread, same_buf, tri_buf, sems, w_sems,
 ):
     rows, width = x_ref.shape
     heads = q_ref.shape[0]
     hd = width // heads
     blocks = rows // BLOCK
-    cols = w_sems.shape[0]
     start = lax.axis_index("hist") * rows
-    fetches = [
-        pltpu.make_async_copy(x_hbm.at[0], x_ref, sems.at[0]),
-        pltpu.make_async_copy(ids_hbm, ids_ref, sems.at[1]),
-        pltpu.make_async_copy(bias_hbm, bias_ref, sems.at[2]),
+    fetch_x = pltpu.make_async_copy(x_hbm.at[0], x_ref, sems.at[0])
+    fetch_ids = pltpu.make_async_copy(ids_hbm, ids_ref, sems.at[1])
+    fetch_bias = pltpu.make_async_copy(bias_hbm, bias_ref, sems.at[2])
+    cut = 2 * width
+    fetch_w = [
+        pltpu.make_async_copy(
+            w_hbm.at[:, i * cut : (i + 1) * cut], w_ref.at[:, i * cut : (i + 1) * cut], w_sems.at[i]
+        )
+        for i in range(2)
     ]
-    step = w_hbm.shape[1] // cols
-    w_fetches = [
-        pltpu.make_async_copy(
-            w_hbm.at[:, c * step : (c + 1) * step], w_ref.at[:, c * step : (c + 1) * step], w_sems.at[c]
-        )
-        for c in range(cols)
-    ]
-    for copy in fetches[:1] + w_fetches + fetches[1:]:
+    for copy in (fetch_ids, fetch_bias, fetch_x, *fetch_w):
         copy.start()
-    fetches[0].wait()
-    scale = 0.5 / math.sqrt(hd)
-    for c in range(cols):
-        w_fetches[c].wait()
-        at = c * step
+    row = lax.broadcasted_iota(jnp.int32, (BLOCK, BLOCK), 0)
+    col = lax.broadcasted_iota(jnp.int32, (BLOCK, BLOCK), 1)
+    tri_buf[...] = jnp.where(col <= row, 1.0, 0.0).astype(jnp.bfloat16)
+    fetch_ids.wait()
+    fetch_bias.wait()
+    mark_same(ids_ref, ids_ref, spread, same_buf, [range(c, blocks) for c in range(blocks)])
+    fetch_x.wait()
+    x_ref[...] = x_ref[...] * jnp.bfloat16(0.5)
+
+    def emit(at, y):
         kind, at = at // width, at % width
-        for r in range(0, rows, M):
-            rs = slice(r, r + M)
-            y = silu(mm(x_ref[rs, :], w_ref[:, c * step : (c + 1) * step]))
-            if kind == 0:
-                gate_ref[rs, at : at + step] = y
-                continue
-            if kind == 1:
-                pos = start + r + lax.broadcasted_iota(jnp.int32, (M, 1), 0)
-                y = jnp.where(pos < length_ref[0], y, 0.0)
-            if kind == 2:
-                y = y.astype(jnp.bfloat16).astype(jnp.float32) * scale
-            y = y.astype(jnp.bfloat16)
-            buf = (None, v_buf, q_ref, k_buf)[kind]
-            for h in range(step // hd):
-                buf[at // hd + h, rs, :] = y[:, h * hd : (h + 1) * hd]
-    for copy in fetches[1:]:
-        copy.wait()
-    spread_ids(ids_ref, qid_buf)
-    keep = triangle()
-
-    def head(h, carry):
-        def store(r, acc):
-            part_ref[h, part(r), :] = acc
-
-        attend(
-            [(r, range(r + 1)) for r in range(blocks)],
-            lambda r: q_ref[h, part(r), :], lambda c: k_buf[h, part(c), :], lambda c: v_buf[h, part(c), :],
-            lambda r: qid_buf[part(r), :], lambda c: ids_ref[:, part(c)], 0.5 * bias_ref[h],
-            lambda r, c: keep if r == c else None, lambda r: None, store,
-        )
-        return carry
-
-    lax.fori_loop(0, heads, head, 0)
+        if kind == 0:
+            gate_ref[:, at : at + y.shape[1]] = y
+        elif kind == 1:
+            pos = start + lax.broadcasted_iota(jnp.int32, (rows, 1), 0)
+            put_heads(v_buf, at, jnp.where(pos < length_ref[0], y, 0.0), hd)
+        elif kind == 2:
+            put_heads(q_ref, at, y * (0.5 / math.sqrt(hd)), hd)
+        else:
+            put_heads(k_buf, at, y, hd)
+
+    for i in range(2):
+        fetch_w[i].wait()
+        columns(x_ref, w_ref, i * cut, cut, 256, emit)
+    for h in range(heads):
+        bias = 0.5 * bias_ref[h]
+        for c in range(blocks):
+            rs = slice(c * BLOCK, rows)
+            half = lax.dot_general(q_ref[h, rs, :], k_buf[h, part(c), :], NT, preferred_element_type=jnp.float32)
+            weights = weigh(half, same_buf[rs, part(c)], bias)
+            edge = weights[:BLOCK] * tri_buf[...]
+            if c < blocks - 1:
+                edge = jnp.concatenate([edge, weights[BLOCK:]], axis=0)
+            term = mm(edge, v_buf[h, part(c), :])
+            part_ref[h, rs, :] = term if c == 0 else part_ref[h, rs, :] + term
 
 
 def halo_kernel(
-    length_ref, bias_ref, x_ref, w_ref, ids_ref, own_ids_ref, events_ref, gate_ref, q_ref, part_ref, w_out_ref,
-    out_ref, k_buf, v_buf, qid_buf, mix_buf, gated_buf,
+    length_ref, bias_ref, halo_ref, w_ref, ids_ref, own_ids_ref, events_ref, gate_ref, q_ref, part_ref, w_out_ref,
+    out_ref, x_ref, k_buf, v_buf, spread, same_buf, tri_buf, mix_buf, gated_buf,
 ):
     rows, width = x_ref.shape
     heads = q_ref.shape[0]
     hd = width // heads
     blocks = rows // BLOCK
     length, start = length_ref[0], lax.axis_index("hist") * rows
-    spread_ids(own_ids_ref, qid_buf)
-    step = 256
-    for kind, buf in ((1, v_buf), (3, k_buf)):
-        for at in range(0, width, step):
-            for r in range(0, rows, M):
-                rs = slice(r, r + M)
-                y = silu(mm(x_ref[rs, :], w_ref[:, kind * width + at : kind * width + at + step]))
-                if kind == 1:
-                    pos = start - WINDOW + r + lax.broadcasted_iota(jnp.int32, (M, 1), 0)
-                    y = jnp.where((pos >= 0) & (pos < length), y, 0.0)
-                y = y.astype(jnp.bfloat16)
-                for h in range(step // hd):
-                    buf[at // hd + h, rs, :] = y[:, h * hd : (h + 1) * hd]
-    keep = jnp.logical_not(triangle())
-
-    def head(h, carry):
-        def store(r, acc):
-            mix_buf[h, part(r), :] = acc
-
-        attend(
-            [(r, range(r, blocks)) for r in range(blocks)],
-            lambda r: q_ref[h, part(r), :], lambda c: k_buf[h, part(c), :], lambda c: v_buf[h, part(c), :],
-            lambda r: qid_buf[part(r), :], lambda c: ids_ref[:, part(c)], 0.5 * bias_ref[h],
-            lambda r, c: keep if r == c else None, lambda r: part_ref[h, part(r), :], store,
-        )
-        return carry
-
-    lax.fori_loop(0, heads, head, 0)
+    row = lax.broadcasted_iota(jnp.int32, (BLOCK, BLOCK), 0)
+    col = lax.broadcasted_iota(jnp.int32, (BLOCK, BLOCK), 1)
+    tri_buf[...] = jnp.where(col > row, 1.0, 0.0).astype(jnp.bfloat16)
+    x_ref[...] = halo_ref[...] * jnp.bfloat16(0.5)
+    mark_same(own_ids_ref, ids_ref, spread, same_buf, [range(c + 1) for c in range(blocks)])
+
+    def emit(at, y):
+        kind, at = at // width, at % width
+        if kind == 1:
+            pos = start - WINDOW + lax.broadcasted_iota(jnp.int32, (rows, 1), 0)
+            put_heads(v_buf, at, jnp.where((pos >= 0) & (pos < length), y, 0.0), hd)
+        else:
+            put_heads(k_buf, at, y, hd)
+
+    columns(x_ref, w_ref, width, width, 256, emit)
+    columns(x_ref, w_ref, 3 * width, width, 256, emit)
+    for h in range(heads):
+        bias = 0.5 * bias_ref[h]
+        for c in range(blocks - 1, -1, -1):
+            rs = slice(0, (c + 1) * BLOCK)
+            half = lax.dot_general(q_ref[h, rs, :], k_buf[h, part(c), :], NT, preferred_element_type=jnp.float32)
+            weights = weigh(half, same_buf[rs, part(c)], bias)
+            edge = weights[c * BLOCK :] * tri_buf[...]
+            if c:
+                edge = jnp.concatenate([weights[: c * BLOCK], edge], axis=0)
+            term = mm(edge, v_buf[h, part(c), :])
+            mix_buf[h, rs, :] = (part_ref if c == blocks - 1 else mix_buf)[h, rs, :] + term
 
     def norm_rows(b, carry):
         rs = pl.ds(pl.multiple_of(b * NORM_ROWS, NORM_ROWS), NORM_ROWS)
@@ -188,16 +170,17 @@
     counted = jnp.where(place < length, 1.0, 0.0).astype(jnp.bfloat16)
     gated_sum = mm(counted, gated_buf[...])
     event_sum = mm(counted, events_ref[...])
-    projected = jnp.dot(
-        gated_sum, w_out_ref[...].astype(jnp.float32),
-        preferred_element_type=jnp.float32, precision=lax.Precision.HIGHEST,
-    )
-    total = (projected + event_sum)[:1]
+    high = gated_sum.astype(jnp.bfloat16).astype(jnp.float32)
+    middle = (gated_sum - high).astype(jnp.bfloat16).astype(jnp.float32)
+    low = gated_sum - high - middle
+    which = lax.broadcasted_iota(jnp.int32, gated_sum.shape, 0)
+    terms = jnp.where(which == 0, high, jnp.where(which == 1, middle, jnp.where(which == 2, low, 0.0)))
+    projected = jnp.sum(mm(terms.astype(jnp.bfloat16), w_out_ref[...]), axis=0, keepdims=True)
+    total = projected + event_sum[:1]
     for j in range(out_ref.shape[0]):
         out_ref[j] = total
 
 
-M = 512
 NORM_ROWS = 32
 NORM_UNROLL = 4
 SMEM = pl.BlockSpec(memory_space=pltpu.SMEM)
@@ -211,7 +194,6 @@
     _, rows, width = events.shape
     heads = bias.shape[0]
     hd = width // heads
-    cols = 4
     return pl.pallas_call(
         own_kernel,
         out_shape=(
@@ -229,8 +211,10 @@
             pltpu.VMEM((heads, rows, hd), jnp.bfloat16),
             pltpu.VMEM((heads, rows, hd), jnp.bfloat16),
             pltpu.VMEM((rows, 128), jnp.int32),
+            pltpu.VMEM((rows, rows), jnp.float32),
+            pltpu.VMEM((BLOCK, BLOCK), jnp.bfloat16),
             pltpu.SemaphoreType.DMA((3,)),
-            pltpu.SemaphoreType.DMA((cols,)),
+            pltpu.SemaphoreType.DMA((2,)),
         ],
         compiler_params=pltpu.CompilerParams(vmem_limit_bytes=26 << 20),
         cost_estimate=pl.CostEstimate(flops=8 * 10**9, bytes_accessed=10**7, transcendentals=4 * 10**6),
@@ -248,9 +232,12 @@
         in_specs=[SMEM, SMEM] + [VMEM] * 9,
         out_specs=VMEM,
         scratch_shapes=[
+            pltpu.VMEM((rows, width), jnp.bfloat16),
             pltpu.VMEM((heads, rows, hd), jnp.bfloat16),
             pltpu.VMEM((heads, rows, hd), jnp.bfloat16),
             pltpu.VMEM((rows, 128), jnp.int32),
+            pltpu.VMEM((rows, rows), jnp.float32),
+            pltpu.VMEM((BLOCK, BLOCK), jnp.bfloat16),
             pltpu.VMEM((heads, rows, hd), jnp.float32),
             pltpu.VMEM((rows, width), jnp.bfloat16),
         ],

time: 99.3 us -> 97.2 us (0.979)
  Pallas kernels: 21.9 us -> 16.1 us
  waiting for transfers between devices: 0.01 us -> 2.06 us
  blocking collectives: 68.3 us -> 70 us
    pallas_call x1, Pallas kernels: 11.1 us -> 7.35 us  [own_part(): pl.pallas_call(own_kernel, out_shape=(jax.ShapeDtypeStruct((rows, width),...]
    pallas_call x1, Pallas kernels: 9.12 us -> 7.01 us  [halo_part(): pl.pallas_call(halo_kernel, out_shape=jax.ShapeDtypeStruct((copies, 1, wi...]
    ppermute x2, waiting for transfers between devices: 0.01 us -> 2.06 us  [shifted(): return lax.ppermute(block, axis, route)]
    all_to_all x4, blocking collectives: 68.3 us -> 70 us  [swapped(): return lax.all_to_all(x, axis, 0, 0, tiled=True)]
  transfers between devices with their start and end apart: 2 -> 2, of which waited for: 0 -> 1; matrix products, arithmetic and copies ran while one was open for 0% -> 0% of each run, Pallas kernels for 11% -> 8%
where the time goes in v3:
time: 97.2 us; the launch traced here: 96.9 us
  blocking collectives  70 us (72%)
  Pallas kernels  16.1 us (17%)
  starting transfers between devices  7.94 us (8%)
  waiting for transfers between devices  2.06 us (2%)
    all_to_all x4, blocking collectives, swapped(): return lax.all_to_all(x, axis, 0, 0, tiled=True)  70 us
    ppermute x2, starting transfers between devices, shifted(): return lax.ppermute(block, axis, route)  7.94 us
    pallas_call x1, Pallas kernels, own_part(): pl.pallas_call(own_kernel, out_shape=(jax.ShapeDtypeStruct((rows, width),...  7.35 us
    pallas_call x1, Pallas kernels, halo_part(): pl.pallas_call(halo_kernel, out_shape=jax.ShapeDtypeStruct((copies, 1, wi...  7.01 us
    ppermute x2, waiting for transfers between devices, shifted(): return lax.ppermute(block, axis, route)  2.06 us
  transfers between devices with their start and end apart: 2, of which 1 were waited for; matrix products, arithmetic and copies ran while one was open for 0% of the time, Pallas kernels for 8%

profile of v3, /device:TPU:1, one launch (start us, length us, event | category | flops | bytes accessed | tf_op | source)
XLA Modules:
  0.0 96.9 jit_solution(11433097882720173603)
XLA Ops:
  0.0 6.0 %collective-permute-start = (bf16[1024,512]{1,0:T(8,128)(2,1)}, bf16[1024,512]{1,0:T(8,128)(2,1)S(1)}, u32[]{:S(2)}, u32[]{:S(2)}) collective-permute-start(bf16[1024,512]{1,0:T(8,128)(2,1)} %bitcast.1), channel_id=1, source_target_pairs={{0,32},{32,64},{64,96},{96,128},{128,160},{160,192},{192,224},{224... | collective-permute-start | bytes 3145736 | tf_op jit(solution)/shard_map/ppermute | solution.py:252
  6.0 1.9 %collective-permute-start.1 = (s32[1,1024]{1,0:T(1,128)}, s32[1,1024]{1,0:T(1,128)S(1)}, u32[]{:S(2)}, u32[]{:S(2)}) collective-permute-start(s32[1,1024]{1,0:T(1,128)} %own_ids_ref.1), channel_id=1, source_target_pairs={{0,32},{32,64},{64,96},{96,128},{128,160},{160,192},{192,224},{224... | collective-permute-start | bytes 12296 | tf_op jit(solution)/shard_map/ppermute | solution.py:252
  8.6 0.0 copy-start
  8.6 0.0 copy-start.1
  8.6 0.0 copy-start.3
  8.6 0.0 copy-start.4
  8.6 0.0 copy-start.5
  8.6 7.3 %own_part.1 = (f32[1024,512]{1,0:T(8,128)S(1)}, bf16[4,1024,128]{2,1,0:T(8,128)(2,1)S(1)}, f32[4,1024,128]{2,1,0:T(8,128)S(1)}) custom-call(bf16[1,1024,512]{2,1,0:T(8,128)(2,1)} %x_hbm.1, bf16[512,2048]{1,0:T(8,128)(2,1)} %w_ref.1, s32[1,1024]{1,0:T(1,128)} %own_ids_ref.1, f32[4]{0:T(128)} %bias_ref.1, s32[1]{0:T(128)S(6)} %copy.8.length_ref), custom_call_target="tpu_custom_call" | custom-call | flops 8000000000 | bytes 10000000 | tf_op jit(solution)/shard_map/own_part/pallas_call | solution.py:197
  16.0 2.1 %collective-permute-done.1.ids_ref = s32[1,1024]{1,0:T(1,128)S(1)} collective-permute-done((s32[1,1024]{1,0:T(1,128)}, s32[1,1024]{1,0:T(1,128)S(1)}, u32[]{:S(2)}, u32[]{:S(2)}) %collective-permute-start.1) | collective-permute-done | bytes 4128 | tf_op jit(solution)/shard_map/ppermute | solution.py:252
  18.1 0.0 collective-permute-done.halo_ref
  18.1 0.0 copy-done
  18.1 0.0 copy-done.1
  18.1 0.0 copy-done.3
  18.1 0.0 copy-done.4
  18.1 0.0 copy-done.5
  18.1 0.0 copy-start.2
  18.1 7.0 %halo_part.1 = f32[16,1,512]{2,1,0:T(1,128)S(1)} custom-call(s32[1]{0:T(128)S(6)} %copy.8.length_ref, f32[4]{0:T(128)S(1)} %copy-done.5, bf16[1024,512]{1,0:T(8,128)(2,1)S(1)} %collective-permute-done.halo_ref, bf16[512,2048]{1,0:T(8,128)(2,1)S(1)} %copy-done, s32[1,1024]{1,0:T(1,128)S(1)} %collective-permute-done.1.ids_ref, s32[1,1024]{1,0:T(1,128)S(1)} %copy-done.4, ...), custom_call_target="tpu_custom_call" | custom-call | tf_op jit(solution)/shard_map/halo_part/pallas_call | solution.py:229
  25.1 15.3 %all_to_all.20.parts_ref = f32[16,1,512]{2,1,0:T(1,128)S(1)} all-to-all(f32[16,1,512]{2,1,0:T(1,128)S(1)} %halo_part.1), channel_id=1, replica_groups=mesh['hist'=16,'item'=32] {'hist'}, dimensions={0} | all-to-all | bytes 65536 | tf_op jit(solution)/shard_map/all_to_all | solution.py:325
  40.5 0.1 vectors.1
  40.6 27.6 %all_to_all.21.vecs_ref = f32[32,1,512]{2,1,0:T(1,128)S(1)} all-to-all(f32[32,1,512]{2,1,0:T(1,128)S(1)} %vectors.1), channel_id=1, replica_groups=mesh['hist'=16,'item'=32] {'item'}, dimensions={0} | all-to-all | bytes 131072 | tf_op jit(solution)/shard_map/all_to_all | solution.py:325
  68.2 0.0 copy-done.2
  68.2 0.7 logits.1
  68.9 12.0 %all_to_all.22.parts_ref = f32[16,1,128]{2,1,0:T(1,128)S(1)} all-to-all(f32[16,1,128]{2,1,0:T(1,128)S(1)} %get-tuple-element.13), channel_id=1, replica_groups=mesh['hist'=16,'item'=32] {'hist'}, dimensions={0} | all-to-all | bytes 16384 | tf_op jit(solution)/shard_map/all_to_all | solution.py:325
  80.9 0.1 join.1
  80.9 15.1 %all_to_all.23.parts_ref = f32[32,1,128]{2,1,0:T(1,128)S(1)} all-to-all(f32[32,1,128]{2,1,0:T(1,128)S(1)} %join.1), channel_id=1, replica_groups=mesh['hist'=16,'item'=32] {'item'}, dimensions={0} | all-to-all | bytes 32768 | tf_op jit(solution)/shard_map/all_to_all | solution.py:325
  96.0 0.9 final.1
Async XLA Ops:
  0.0 18.1 %collective-permute-start = (bf16[1024,512]{1,0:T(8,128)(2,1)}, bf16[1024,512]{1,0:T(8,128)(2,1)S(1)}, u32[]{:S(2)}, u32[]{:S(2)}) collective-permute-start(bf16[1024,512]{1,0:T(8,128)(2,1)} %bitcast.1), channel_id=1, source_target_pairs={{0,32},{32,64},{64,96},{96,128},{128,160},{160,192},{192,224},{224... | collective-permute-start | bytes 3145736 | tf_op jit(solution)/shard_map/ppermute | solution.py:252
  6.0 12.0 %collective-permute-start.1 = (s32[1,1024]{1,0:T(1,128)}, s32[1,1024]{1,0:T(1,128)S(1)}, u32[]{:S(2)}, u32[]{:S(2)}) collective-permute-start(s32[1,1024]{1,0:T(1,128)} %own_ids_ref.1), channel_id=1, source_target_pairs={{0,32},{32,64},{64,96},{96,128},{128,160},{160,192},{192,224},{224... | collective-permute-start | bytes 12296 | tf_op jit(solution)/shard_map/ppermute | solution.py:252
  8.6 9.5 %copy-start = (bf16[512,2048]{1,0:T(8,128)(2,1)S(1)}, bf16[512,2048]{1,0:T(8,128)(2,1)}, u32[]{:S(2)}) copy-start(bf16[512,2048]{1,0:T(8,128)(2,1)} %w_ref.1) | copy-start | bytes 6291460
  8.6 9.5 %copy-start.1 = (bf16[1,1024,512]{2,1,0:T(8,128)(2,1)S(1)}, bf16[1,1024,512]{2,1,0:T(8,128)(2,1)}, u32[]{:S(2)}) copy-start(bf16[1,1024,512]{2,1,0:T(8,128)(2,1)} %x_hbm.1) | copy-start | bytes 3145732
  8.6 9.5 %copy-start.3 = (bf16[512,512]{1,0:T(8,128)(2,1)S(1)}, bf16[512,512]{1,0:T(8,128)(2,1)}, u32[]{:S(2)}) copy-start(bf16[512,512]{1,0:T(8,128)(2,1)} %w_out_ref.1) | copy-start | bytes 1572868
  8.6 9.5 %copy-start.4 = (s32[1,1024]{1,0:T(1,128)S(1)}, s32[1,1024]{1,0:T(1,128)}, u32[]{:S(2)}) copy-start(s32[1,1024]{1,0:T(1,128)} %own_ids_ref.1) | copy-start | bytes 12292
  8.6 9.5 %copy-start.5 = (f32[4]{0:T(128)S(1)}, f32[4]{0:T(128)}, u32[]{:S(2)}) copy-start(f32[4]{0:T(128)} %bias_ref.1) | copy-start | bytes 52
  18.1 50.1 %copy-start.2 = (bf16[1024,512]{1,0:T(8,128)(2,1)S(1)}, bf16[1024,512]{1,0:T(8,128)(2,1)}, u32[]{:S(2)}) copy-start(bf16[1024,512]{1,0:T(8,128)(2,1)} %slab_ref.1) | copy-start | bytes 3145732

commit v4 on v3

v4 whole, which is shorter than its diff:
```python
import functools
import math

import jax
import jax.numpy as jnp
from jax import lax
from jax.experimental import pallas as pl
from jax.experimental.pallas import tpu as pltpu
from jax.sharding import PartitionSpec as P


WINDOW = 1024
BLOCK = 256
NT = (((1,), (1,)), ((), ()))


def mm(a, b):
    return jnp.dot(a, b, preferred_element_type=jnp.float32)


def spread_ids(row, out_ref):
    for b in range(out_ref.shape[0] // 128):
        out_ref[b * 128 : (b + 1) * 128, :] = jnp.broadcast_to(row[:, b * 128 : (b + 1) * 128], (128, 128)).T


def part(b):
    return slice(b * BLOCK, (b + 1) * BLOCK)


def mark_same(spread, rows, ids):
    mine = jnp.concatenate([spread[rows, :]] * (ids.shape[1] // 128), axis=1)
    return jnp.where(mine == ids, 1.0, 0.0)


def triangle(below):
    row = lax.broadcasted_iota(jnp.int32, (BLOCK, BLOCK), 0)
    col = lax.broadcasted_iota(jnp.int32, (BLOCK, BLOCK), 1)
    return jnp.where((col <= row) if below else (col > row), 1.0, 0.0).astype(jnp.bfloat16)


def mixed_term(q, k, v, same, bias, tri, at):
    half = lax.dot_general(q, k, NT, preferred_element_type=jnp.float32) + same * bias
    weights = (half * jnp.tanh(half) + half).astype(jnp.bfloat16)
    pieces = [weights[:at], weights[at : at + BLOCK] * tri, weights[at + BLOCK :]]
    pieces = [p for p in pieces if p.shape[0]]
    return mm(jnp.concatenate(pieces, axis=0) if len(pieces) > 1 else pieces[0], v)


def columns(x_ref, w_ref, first, count, emit, base=0):
    for at in range(first, first + count, 256):
        half = mm(x_ref[...], w_ref[:, at - base : at - base + 256])
        emit(at, half * jnp.tanh(half) + half)


def put_heads(buf, at, y, hd):
    y = y.astype(jnp.bfloat16)
    for h in range(y.shape[1] // hd):
        buf[at // hd + h] = y[:, h * hd : (h + 1) * hd]


def digit_rows(ids):
    which = lax.broadcasted_iota(jnp.int32, (16, ids.shape[1]), 0)
    digits = jnp.where(which == 0, ids & 127, jnp.where(which == 1, (ids >> 7) & 127, ids >> 14))
    return jnp.where(which < 3, digits, 0).astype(jnp.float32).astype(jnp.bfloat16)


def from_digits(rows):
    rows = rows.astype(jnp.float32)
    return (rows[0:1] + 128.0 * rows[1:2] + 16384.0 * rows[2:3]).astype(jnp.int32)


def start_kernel(
    x_hbm, w_hbm, ids_hbm, length_ref, high_ref, low_ref, x_ref, gate_ref, v_ref, spread_ref, events_ref,
    w_ref, ids_ref, sems,
):
    rows, width = x_ref.shape
    hd = v_ref.shape[2]
    cut = rows // 2
    start = lax.axis_index("hist") * rows
    copies = [
        pltpu.make_async_copy(ids_hbm, ids_ref, sems.at[0]),
        pltpu.make_async_copy(x_hbm.at[0], events_ref, sems.at[1]),
        pltpu.make_async_copy(w_hbm.at[:, : 2 * width], w_ref, sems.at[2]),
    ]
    for copy in copies:
        copy.start()
    copies[0].wait()
    ids = ids_ref[...]
    spread_ids(ids, spread_ref)
    low_ref[cut:, :] = digit_rows(ids[:, :cut])
    high_ref[cut:, :] = digit_rows(ids[:, cut:])
    copies[1].wait()
    low_ref[:cut, :] = events_ref[:cut, :]
    high_ref[:cut, :] = events_ref[cut:, :]
    x_ref[...] = events_ref[...] * jnp.bfloat16(0.5)
    copies[2].wait()

    def emit(at, y):
        if at < width:
            gate_ref[:, at : at + y.shape[1]] = y
        else:
            pos = start + lax.broadcasted_iota(jnp.int32, (rows, 1), 0)
            put_heads(v_ref, at - width, jnp.where(pos < length_ref[0], y, 0.0), hd)

    columns(x_ref, w_ref, 0, 2 * width, emit)


def own_kernel(bias_ref, x_ref, w_ref, ids_ref, spread_ref, v_ref, q_ref, part_ref, k_buf, same_buf):
    rows, width = x_ref.shape
    heads, _, hd = v_ref.shape
    blocks = rows // BLOCK
    tri = triangle(True)
    for c in range(blocks):
        same_buf[c * BLOCK :, part(c)] = mark_same(spread_ref, slice(c * BLOCK, rows), ids_ref[:, part(c)])

    def emit(at, y):
        if at < 3 * width:
            put_heads(q_ref, at - 2 * width, y * (0.5 / math.sqrt(hd)), hd)
        else:
            put_heads(k_buf, at - 3 * width, y, hd)

    columns(x_ref, w_ref, 2 * width, 2 * width, emit)
    for h in range(heads):
        for c in range(blocks):
            rs = slice(c * BLOCK, rows)
            term = mixed_term(
                q_ref[h, rs, :], k_buf[h, part(c), :], v_ref[h, part(c), :], same_buf[rs, part(c)],
                0.5 * bias_ref[h], tri, 0,
            )
            part_ref[h, rs, :] = term if c == 0 else part_ref[h, rs, :] + term


def halo_piece(first, length, bias_ref, got_ref, w_ref, spread_ref, q_ref, part_ref, x_buf, k_buf, v_buf, same_buf, mix_ref):
    heads, _, hd = q_ref.shape
    keys, width = x_buf.shape
    blocks = keys // BLOCK
    tri = triangle(False)
    x_buf[...] = got_ref[:keys, :] * jnp.bfloat16(0.5)
    ids = from_digits(got_ref[keys:, :])
    for c in range(blocks):
        end = (first + c + 1) * BLOCK
        same_buf[:end, part(c)] = mark_same(spread_ref, slice(0, end), ids[:, part(c)])
    pos = lax.axis_index("hist") * WINDOW - WINDOW + first * BLOCK + lax.broadcasted_iota(jnp.int32, (keys, 1), 0)

    def emit(at, y):
        if at < 2 * width:
            put_heads(v_buf, at - width, jnp.where((pos >= 0) & (pos < length), y, 0.0), hd)
        else:
            put_heads(k_buf, at - 3 * width, y, hd)

    columns(x_buf, w_ref, width, width, emit)
    columns(x_buf, w_ref, 3 * width, width, emit)
    for h in range(heads):
        for c in range(blocks - 1, -1, -1):
            rs = slice(0, (first + c + 1) * BLOCK)
            term = mixed_term(
                q_ref[h, rs, :], k_buf[h, part(c), :], v_buf[h, part(c), :], same_buf[rs, part(c)],
                0.5 * bias_ref[h], tri, (first + c) * BLOCK,
            )
            mix_ref[h, rs, :] = (part_ref if c == blocks - 1 else mix_ref)[h, rs, :] + term


def gated_sum(first, rows, length, mix_ref, gate_ref, gated_buf):
    heads, _, hd = mix_ref.shape
    width = heads * hd

    def norm_rows(b, carry):
        at = pl.multiple_of(b * NORM_ROWS, NORM_ROWS)
        rs = pl.ds(first + at, NORM_ROWS)
        mixed = [mix_ref[h, rs, :] for h in range(heads)]
        mean = jnp.sum(sum(mixed), axis=1, keepdims=True) * (1.0 / width)
        mixed = [m - mean for m in mixed]
        spread = jnp.sum(sum(m * m for m in mixed), axis=1, keepdims=True) * (1.0 / width)
        factor = lax.rsqrt(spread + 1e-06 * WINDOW * WINDOW)
        for h in range(heads):
            gated = mixed[h] * factor * gate_ref[rs, h * hd : (h + 1) * hd]
            gated_buf[pl.ds(at, NORM_ROWS), h * hd : (h + 1) * hd] = gated.astype(jnp.bfloat16)
        return carry

    lax.fori_loop(0, rows // NORM_ROWS, norm_rows, 0, unroll=NORM_UNROLL)
    return mm(valid(first, rows, length), gated_buf[...])


def valid(first, rows, length):
    place = lax.axis_index("hist") * WINDOW + first + lax.broadcasted_iota(jnp.int32, (8, rows), 1)
    return jnp.where(place < length, 1.0, 0.0).astype(jnp.bfloat16)


def high_kernel(
    length_ref, bias_ref, got_ref, w_ref, spread_ref, q_ref, part_ref, gate_ref, events_ref,
    mix_ref, sums_ref, x_buf, k_buf, v_buf, same_buf, gated_buf,
):
    rows = q_ref.shape[1]
    cut = rows // 2
    length = length_ref[0]
    halo_piece(
        cut // BLOCK, length, bias_ref, got_ref, w_ref, spread_ref, q_ref, part_ref, x_buf, k_buf, v_buf, same_buf, mix_ref
    )
    sums_ref[0] = gated_sum(cut, rows - cut, length, mix_ref, gate_ref, gated_buf)
    sums_ref[1] = mm(valid(0, rows, length), events_ref[...])


def low_kernel(
    length_ref, bias_ref, got_ref, w_ref, spread_ref, q_ref, part_ref, gate_ref, sums_ref, w_out_ref,
    out_ref, x_buf, k_buf, v_buf, same_buf, mix_buf, gated_buf,
):
    cut = gated_buf.shape[0]
    length = length_ref[0]
    halo_piece(0, length, bias_ref, got_ref, w_ref, spread_ref, q_ref, part_ref, x_buf, k_buf, v_buf, same_buf, mix_buf)
    total = sums_ref[0] + gated_sum(0, cut, length, mix_buf, gate_ref, gated_buf)
    high = total.astype(jnp.bfloat16).astype(jnp.float32)
    middle = (total - high).astype(jnp.bfloat16).astype(jnp.float32)
    low = total - high - middle
    which = lax.broadcasted_iota(jnp.int32, total.shape, 0)
    terms = jnp.where(which == 0, high, jnp.where(which == 1, middle, jnp.where(which == 2, low, 0.0)))
    projected = jnp.sum(mm(terms.astype(jnp.bfloat16), w_out_ref[...]), axis=0, keepdims=True)
    pooled = projected + sums_ref[1][:1]
    for j in range(out_ref.shape[0]):
        out_ref[j] = pooled


NORM_ROWS = 32
NORM_UNROLL = 4


SMEM = pl.BlockSpec(memory_space=pltpu.SMEM)
VMEM = pl.BlockSpec(memory_space=pltpu.VMEM)


def shifted(block, axis, distance):
    devices = range(lax.axis_size(axis))
    route = [(i - distance, i) for i in devices if i - distance in devices]
    return lax.ppermute(block, axis, route)


HBM = pl.BlockSpec(memory_space=pltpu.MemorySpace.HBM)


def kernel_call(kernel, outs, specs, scratch, args, mflops):
    return pl.pallas_call(
        kernel,
        out_shape=outs,
        in_specs=specs,
        out_specs=jax.tree.map(lambda _: VMEM, outs),
        scratch_shapes=scratch,
        compiler_params=pltpu.CompilerParams(vmem_limit_bytes=24 << 20),
        cost_estimate=pl.CostEstimate(flops=mflops * 10**6, bytes_accessed=10**7, transcendentals=10**6),
    )(*args)


def local_pool(events, item_ids, lengths, w_proj, w_out, repeat_bias):
    _, rows, width = events.shape
    heads = repeat_bias.shape[0]
    hd = width // heads
    cut = rows // 2
    bf16 = functools.partial(jax.ShapeDtypeStruct, dtype=jnp.bfloat16)
    f32 = functools.partial(jax.ShapeDtypeStruct, dtype=jnp.float32)
    stay = [pltpu.with_memory_space_constraint(a, pltpu.MemorySpace.HBM) for a in (events, w_proj, item_ids)]
    high, low, x, gate, v, spread, own = kernel_call(
        start_kernel,
        (
            bf16((cut + 16, width)), bf16((cut + 16, width)), bf16((rows, width)), f32((rows, width)),
            bf16((heads, rows, hd)), jax.ShapeDtypeStruct((rows, 128), jnp.int32), bf16((rows, width)),
        ),
        [HBM] * 3 + [SMEM],
        [
            pltpu.VMEM((width, 2 * width), jnp.bfloat16),
            pltpu.VMEM(item_ids.shape, jnp.int32),
            pltpu.SemaphoreType.DMA((3,)),
        ],
        (*stay, lengths), 1000,
    )
    high = shifted(high, "hist", 1)
    low = shifted(low, "hist", 1)
    q, mixed = kernel_call(
        own_kernel,
        (bf16((heads, rows, hd)), f32((heads, rows, hd))),
        [SMEM] + [VMEM] * 5,
        [pltpu.VMEM((heads, rows, hd), jnp.bfloat16), pltpu.VMEM((rows, rows), jnp.float32)],
        (repeat_bias, x, w_proj, item_ids, spread, v), 6000,
    )
    piece = [
        pltpu.VMEM((cut, width), jnp.bfloat16),
        pltpu.VMEM((heads, cut, hd), jnp.bfloat16),
        pltpu.VMEM((heads, cut, hd), jnp.bfloat16),
    ]
    mixed, sums = kernel_call(
        high_kernel,
        (f32((heads, rows, hd)), f32((2, 8, width))),
        [SMEM] * 2 + [VMEM] * 7,
        piece + [pltpu.VMEM((rows, cut), jnp.float32), pltpu.VMEM((cut, width), jnp.bfloat16)],
        (lengths, repeat_bias, high, w_proj, spread, q, mixed, gate, own), 4000,
    )
    return kernel_call(
        low_kernel,
        f32((lax.axis_size("hist"), 1, width)),
        [SMEM] * 2 + [VMEM] * 8,
        piece + [
            pltpu.VMEM((cut, cut), jnp.float32), pltpu.VMEM((heads, cut, hd), jnp.float32),
            pltpu.VMEM((cut, width), jnp.bfloat16),
        ],
        (lengths, repeat_bias, low, w_proj, spread, q, mixed, gate, sums, w_out), 2000,
    )


def vector_kernel(parts_ref, out_ref):
    pooled = parts_ref[0]
    for j in range(1, parts_ref.shape[0]):
        pooled = pooled + parts_ref[j]
    normed = pooled * lax.rsqrt(jnp.mean(pooled * pooled, axis=1, keepdims=True) + 1e-06)
    normed = normed.astype(jnp.bfloat16).astype(jnp.float32)
    for j in range(out_ref.shape[0]):
        out_ref[j] = normed


def as_row(column):
    users = column.shape[0]
    square = jnp.concatenate(
        [jnp.broadcast_to(column, (users, 128)), jnp.zeros((128 - users, 128), jnp.float32)], axis=0
    )
    return square.T[:1]


def logit_kernel(vecs_ref, slab_ref, logits_ref, lse_ref):
    vecs = jnp.concatenate([vecs_ref[j] for j in range(vecs_ref.shape[0])], axis=0).astype(jnp.bfloat16)
    logits = 4.0 * lax.dot_general(vecs, slab_ref[...], NT, preferred_element_type=jnp.float32)
    logits_ref[...] = logits
    top = jnp.max(logits, axis=1, keepdims=True)
    lse = top + jnp.log(jnp.sum(jnp.exp(logits - top), axis=1, keepdims=True))
    row = as_row(lse)
    for j in range(lse_ref.shape[0]):
        lse_ref[j] = row


def joined(parts_ref):
    parts = [parts_ref[j] for j in range(parts_ref.shape[0])]
    top = functools.reduce(jnp.maximum, parts)
    return top + jnp.log(sum(jnp.exp(p - top) for p in parts))


def join_kernel(parts_ref, out_ref):
    lse = joined(parts_ref)
    for j in range(out_ref.shape[0]):
        out_ref[j] = lse


def final_kernel(parts_ref, logits_ref, out_ref):
    users = logits_ref.shape[0]
    lse = jnp.broadcast_to(joined(parts_ref), (128, 128)).T[:users, :1]
    out_ref[...] = logits_ref[...] - lse


def small(kernel, outs, *args):
    return pl.pallas_call(
        kernel,
        out_shape=outs,
        in_specs=[VMEM] * len(args),
        out_specs=jax.tree.map(lambda _: VMEM, outs),
        compiler_params=pltpu.CompilerParams(vmem_limit_bytes=16 << 20),
    )(*args)


def swapped(x, axis):
    return lax.all_to_all(x, axis, 0, 0, tiled=True)


def local(events, item_ids, lengths, w_proj, w_out, repeat_bias, item_slab):
    f32 = functools.partial(jax.ShapeDtypeStruct, dtype=jnp.float32)
    hists, items = lax.axis_size("hist"), lax.axis_size("item")
    users, width = items * events.shape[0], events.shape[2]
    parts = local_pool(events, item_ids, lengths, w_proj, w_out, repeat_bias)
    vecs = small(vector_kernel, f32((items, 1, width)), swapped(parts, "hist"))
    logits, lse = small(
        logit_kernel, (f32((users, item_slab.shape[0])), f32((hists, 1, 128))),
        swapped(vecs, "item"), item_slab,
    )
    lse = small(join_kernel, f32((items, 1, 128)), swapped(lse, "hist"))
    return small(final_kernel, f32(logits.shape), swapped(lse, "item"), logits)


def solution(mesh):
    placed = (
        P("item", "hist", None),
        P("item", "hist"),
        P("item"),
        P(),
        P(),
        P(),
        P(("hist", "item"), None),
    )
    return jax.shard_map(
        local, mesh=mesh, in_specs=placed, out_specs=P(None, ("hist", "item")), check_vma=False
    )
```

time: 97.2 us -> 102 us (1.049)
  waiting for transfers between devices: 2.06 us -> 5.38 us
  Pallas kernels: 16.1 us -> 17.5 us
    ppermute x2, waiting for transfers between devices: 2.06 us -> 5.38 us  [shifted(): return lax.ppermute(block, axis, route)]
    pallas_call x2 -> x4, Pallas kernels: 14.4 us -> 15.8 us  [kernel_call(): pl.pallas_call(kernel, out_shape=outs, in_specs=specs, out_specs=jax.tree...]
  transfers between devices with their start and end apart: 2 -> 2, of which waited for: 1 -> 1; matrix products, arithmetic and copies ran while one was open for 0% -> 0% of each run, Pallas kernels for 8% -> 9%
where the time goes in v4:
time: 102 us
  blocking collectives  70.1 us (69%)
  Pallas kernels  17.5 us (17%)
  starting transfers between devices  7.95 us (8%)
  waiting for transfers between devices  5.38 us (5%)
    all_to_all x4, blocking collectives, swapped(): return lax.all_to_all(x, axis, 0, 0, tiled=True)  70.1 us
    pallas_call x4, Pallas kernels, kernel_call(): pl.pallas_call(kernel, out_shape=outs, in_specs=specs, out_specs=jax.tree...  15.8 us
    ppermute x2, starting transfers between devices, shifted(): return lax.ppermute(block, axis, route)  7.95 us
    ppermute x2, waiting for transfers between devices, shifted(): return lax.ppermute(block, axis, route)  5.38 us
  transfers between devices with their start and end apart: 2, of which 1 were waited for; matrix products, arithmetic and copies ran while one was open for 0% of the time, Pallas kernels for 9%

profile of v4, /device:TPU:1, one launch (start us, length us, event | category | flops | bytes accessed | tf_op | source)
XLA Modules:
  0.0 101.9 jit_solution(10324905677016314989)
XLA Ops:
  0.0 0.0 copy-start
  0.0 0.0 copy-start.4
  0.0 0.0 copy-start.3
  0.8 2.9 %shard_map.73 = (bf16[528,512]{1,0:T(8,128)(2,1)S(1)}, bf16[528,512]{1,0:T(8,128)(2,1)S(1)}, bf16[1024,512]{1,0:T(8,128)(2,1)S(1)}, f32[1024,512]{1,0:T(8,128)S(...) custom-call(bf16[1,1024,512]{2,1,0:T(8,128)(2,1)} %x_hbm.1, ...), custom_call_target="tpu_custom_call" | custom-call | flops 1000000000 | bytes 10000000 | tf_op jit(solution)/shard_map/pallas_call | solution.py:240
  3.7 6.0 %collective-permute-start = (bf16[528,512]{1,0:T(8,128)(2,1)S(1)}, bf16[528,512]{1,0:T(8,128)(2,1)S(1)}, u32[]{:S(2)}, u32[]{:S(2)}) collective-permute-start(bf16[528,512]{1,0:T(8,128)(2,1)S(1)} %get-tuple-element.18), channel_id=1, source_target_pairs={{0,32},{32,64},{64,96},{96,128},{128,160},{160,192},{192,224},{224... | collective-permute-start | bytes 1622024 | tf_op jit(solution)/shard_map/ppermute | solution.py:233
  9.8 1.9 %collective-permute-start.1 = (bf16[528,512]{1,0:T(8,128)(2,1)S(1)}, bf16[528,512]{1,0:T(8,128)(2,1)S(1)}, u32[]{:S(2)}, u32[]{:S(2)}) collective-permute-start(bf16[528,512]{1,0:T(8,128)(2,1)S(1)} %get-tuple-element.23), channel_id=1, source_target_pairs={{0,32},{32,64},{64,96},{96,128},{128,160},{160,192},{192,224},{224... | collective-permute-start | bytes 1622024 | tf_op jit(solution)/shard_map/ppermute | solution.py:233
  11.7 0.0 copy-done
  11.7 0.0 copy-done.4
  11.7 0.0 copy-done.3
  11.7 4.7 %shard_map.74 = (bf16[4,1024,128]{2,1,0:T(8,128)(2,1)S(1)}, f32[4,1024,128]{2,1,0:T(8,128)S(1)}) custom-call(f32[4]{0:T(128)S(1)} %copy-done.3, bf16[1024,512]{1,0:T(8,128)(2,1)S(1)} %get-tuple-element.20.x_ref, bf16[512,2048]{1,0:T(8,128)(2,1)S(1)} %copy-done, s32[1,1024]{1,0:T(1,128)S(1)} %copy-done.4, s32[1024,128]{1,0:T(8,128)S(1)} %get-tuple-element.19.spread_ref, ...), custom_call_target="tpu_custom_call" | custom-call | flops 6000000000 | bytes 10000000 | tf_op jit(solution)/shard_map/pallas_call | solution.py:240
  16.5 5.4 %collective-permute-done.1.got_ref = bf16[528,512]{1,0:T(8,128)(2,1)S(1)} collective-permute-done((bf16[528,512]{1,0:T(8,128)(2,1)S(1)}, bf16[528,512]{1,0:T(8,128)(2,1)S(1)}, u32[]{:S(2)}, u32[]{:S(2)}) %collective-permute-start.1) | collective-permute-done | bytes 540704 | tf_op jit(solution)/shard_map/ppermute | solution.py:233
  21.9 0.0 copy-start.2
  21.9 4.6 %shard_map.75 = (f32[4,1024,128]{2,1,0:T(8,128)S(1)}, f32[2,8,512]{2,1,0:T(8,128)S(1)}) custom-call(s32[1]{0:T(128)S(6)} %copy.8.length_ref, f32[4]{0:T(128)S(1)} %copy-done.3, bf16[528,512]{1,0:T(8,128)(2,1)S(1)} %collective-permute-done.1.got_ref, bf16[512,2048]{1,0:T(8,128)(2,1)S(1)} %copy-done, s32[1024,128]{1,0:T(8,128)S(1)} %get-tuple-element.19.spread_ref, ...), custom_call_target="tpu_custom_call" | custom-call | flops 4000000000 | bytes 10000000 | tf_op jit(solution)/shard_map/pallas_call | solution.py:240
  26.5 0.0 collective-permute-done.got_ref
  26.5 0.0 copy-done.2
  26.5 0.0 copy-start.1
  26.5 3.5 %shard_map.76 = f32[16,1,512]{2,1,0:T(1,128)S(1)} custom-call(s32[1]{0:T(128)S(6)} %copy.8.length_ref, f32[4]{0:T(128)S(1)} %copy-done.3, bf16[528,512]{1,0:T(8,128)(2,1)S(1)} %collective-permute-done.got_ref, bf16[512,2048]{1,0:T(8,128)(2,1)S(1)} %copy-done, s32[1024,128]{1,0:T(8,128)S(1)} %get-tuple-element.19.spread_ref, ...), custom_call_target="tpu_custom_call" | custom-call | flops 2000000000 | bytes 10000000 | tf_op jit(solution)/shard_map/pallas_call | solution.py:240
  30.0 15.4 %all_to_all.20.parts_ref = f32[16,1,512]{2,1,0:T(1,128)S(1)} all-to-all(f32[16,1,512]{2,1,0:T(1,128)S(1)} %shard_map.76), channel_id=1, replica_groups=mesh['hist'=16,'item'=32] {'hist'}, dimensions={0} | all-to-all | bytes 65536 | tf_op jit(solution)/shard_map/all_to_all | solution.py:364
  45.4 0.1 shard_map.77
  45.6 27.6 %all_to_all.21.vecs_ref = f32[32,1,512]{2,1,0:T(1,128)S(1)} all-to-all(f32[32,1,512]{2,1,0:T(1,128)S(1)} %shard_map.77), channel_id=1, replica_groups=mesh['hist'=16,'item'=32] {'item'}, dimensions={0} | all-to-all | bytes 131072 | tf_op jit(solution)/shard_map/all_to_all | solution.py:364
  73.2 0.0 copy-done.1
  73.2 0.7 shard_map.78
  73.8 12.0 %all_to_all.22.parts_ref = f32[16,1,128]{2,1,0:T(1,128)S(1)} all-to-all(f32[16,1,128]{2,1,0:T(1,128)S(1)} %get-tuple-element.29), channel_id=1, replica_groups=mesh['hist'=16,'item'=32] {'hist'}, dimensions={0} | all-to-all | bytes 16384 | tf_op jit(solution)/shard_map/all_to_all | solution.py:364
  85.8 0.1 shard_map.79
  85.9 15.1 %all_to_all.23.parts_ref = f32[32,1,128]{2,1,0:T(1,128)S(1)} all-to-all(f32[32,1,128]{2,1,0:T(1,128)S(1)} %shard_map.79), channel_id=1, replica_groups=mesh['hist'=16,'item'=32] {'item'}, dimensions={0} | all-to-all | bytes 32768 | tf_op jit(solution)/shard_map/all_to_all | solution.py:364
  101.0 0.9 shard_map.80
Async XLA Ops:
  0.0 11.7 %copy-start = (bf16[512,2048]{1,0:T(8,128)(2,1)S(1)}, bf16[512,2048]{1,0:T(8,128)(2,1)}, u32[]{:S(2)}) copy-start(bf16[512,2048]{1,0:T(8,128)(2,1)} %w_ref.5) | copy-start | bytes 6291460
  0.0 11.7 %copy-start.4 = (s32[1,1024]{1,0:T(1,128)S(1)}, s32[1,1024]{1,0:T(1,128)}, u32[]{:S(2)}) copy-start(s32[1,1024]{1,0:T(1,128)} %ids_ref.1) | copy-start | bytes 12292
  0.0 11.7 %copy-start.3 = (f32[4]{0:T(128)S(1)}, f32[4]{0:T(128)}, u32[]{:S(2)}) copy-start(f32[4]{0:T(128)} %bias_ref.5) | copy-start | bytes 52
  3.7 22.7 %collective-permute-start = (bf16[528,512]{1,0:T(8,128)(2,1)S(1)}, bf16[528,512]{1,0:T(8,128)(2,1)S(1)}, u32[]{:S(2)}, u32[]{:S(2)}) collective-permute-start(bf16[528,512]{1,0:T(8,128)(2,1)S(1)} %get-tuple-element.18), channel_id=1, source_target_pairs={{0,32},{32,64},{64,96},{96,128},{128,160},{160,192},{192,224},{224... | collective-permute-start | bytes 1622024 | tf_op jit(solution)/shard_map/ppermute | solution.py:233
  9.8 12.1 %collective-permute-start.1 = (bf16[528,512]{1,0:T(8,128)(2,1)S(1)}, bf16[528,512]{1,0:T(8,128)(2,1)S(1)}, u32[]{:S(2)}, u32[]{:S(2)}) collective-permute-start(bf16[528,512]{1,0:T(8,128)(2,1)S(1)} %get-tuple-element.23), channel_id=1, source_target_pairs={{0,32},{32,64},{64,96},{96,128},{128,160},{160,192},{192,224},{224... | collective-permute-start | bytes 1622024 | tf_op jit(solution)/shard_map/ppermute | solution.py:233
  21.9 4.6 %copy-start.2 = (bf16[512,512]{1,0:T(8,128)(2,1)S(1)}, bf16[512,512]{1,0:T(8,128)(2,1)}, u32[]{:S(2)}) copy-start(bf16[512,512]{1,0:T(8,128)(2,1)} %w_out_ref.1) | copy-start | bytes 1572868
  26.5 46.7 %copy-start.1 = (bf16[1024,512]{1,0:T(8,128)(2,1)S(1)}, bf16[1024,512]{1,0:T(8,128)(2,1)}, u32[]{:S(2)}) copy-start(bf16[1024,512]{1,0:T(8,128)(2,1)} %slab_ref.1) | copy-start | bytes 3145732

commit v5 on v4

--- a/solution.py
+++ b/solution.py
@@ -46,9 +46,9 @@
     return mm(jnp.concatenate(pieces, axis=0) if len(pieces) > 1 else pieces[0], v)
 
 
-def columns(x_ref, w_ref, first, count, emit, base=0):
+def columns(x_ref, w_ref, first, count, emit):
     for at in range(first, first + count, 256):
-        half = mm(x_ref[...], w_ref[:, at - base : at - base + 256])
+        half = mm(x_ref[...], w_ref[:, at : at + 256])
         emit(at, half * jnp.tanh(half) + half)
 
 
@@ -69,57 +69,51 @@
     return (rows[0:1] + 128.0 * rows[1:2] + 16384.0 * rows[2:3]).astype(jnp.int32)
 
 
-def start_kernel(
-    x_hbm, w_hbm, ids_hbm, length_ref, high_ref, low_ref, x_ref, gate_ref, v_ref, spread_ref, events_ref,
-    w_ref, ids_ref, sems,
-):
-    rows, width = x_ref.shape
-    hd = v_ref.shape[2]
-    cut = rows // 2
-    start = lax.axis_index("hist") * rows
+def send_kernel(x_hbm, ids_hbm, high_ref, low_ref, events_ref, ids_ref, sems):
+    cut = ids_ref.shape[1] // 2
     copies = [
-        pltpu.make_async_copy(ids_hbm, ids_ref, sems.at[0]),
-        pltpu.make_async_copy(x_hbm.at[0], events_ref, sems.at[1]),
-        pltpu.make_async_copy(w_hbm.at[:, : 2 * width], w_ref, sems.at[2]),
+        pltpu.make_async_copy(x_hbm.at[0, cut:], events_ref.at[cut:], sems.at[0]),
+        pltpu.make_async_copy(x_hbm.at[0, :cut], events_ref.at[:cut], sems.at[1]),
+        pltpu.make_async_copy(ids_hbm, ids_ref, sems.at[2]),
     ]
     for copy in copies:
         copy.start()
+    copies[2].wait()
+    ids = ids_ref[...]
+    high_ref[cut:, :] = digit_rows(ids[:, cut:])
+    low_ref[cut:, :] = digit_rows(ids[:, :cut])
     copies[0].wait()
-    ids = ids_ref[...]
-    spread_ids(ids, spread_ref)
-    low_ref[cut:, :] = digit_rows(ids[:, :cut])
-    high_ref[cut:, :] = digit_rows(ids[:, cut:])
+    high_ref[:cut, :] = events_ref[cut:, :]
     copies[1].wait()
     low_ref[:cut, :] = events_ref[:cut, :]
-    high_ref[:cut, :] = events_ref[cut:, :]
-    x_ref[...] = events_ref[...] * jnp.bfloat16(0.5)
-    copies[2].wait()
-
-    def emit(at, y):
-        if at < width:
-            gate_ref[:, at : at + y.shape[1]] = y
-        else:
-            pos = start + lax.broadcasted_iota(jnp.int32, (rows, 1), 0)
-            put_heads(v_ref, at - width, jnp.where(pos < length_ref[0], y, 0.0), hd)
-
-    columns(x_ref, w_ref, 0, 2 * width, emit)
-
-
-def own_kernel(bias_ref, x_ref, w_ref, ids_ref, spread_ref, v_ref, q_ref, part_ref, k_buf, same_buf):
-    rows, width = x_ref.shape
+
+
+def own_kernel(
+    length_ref, bias_ref, events_ref, w_ref, ids_ref, gate_ref, v_ref, spread_ref, q_ref, part_ref,
+    x_buf, k_buf, same_buf,
+):
+    rows, width = x_buf.shape
     heads, _, hd = v_ref.shape
     blocks = rows // BLOCK
     tri = triangle(True)
+    spread_ids(ids_ref[...], spread_ref)
     for c in range(blocks):
         same_buf[c * BLOCK :, part(c)] = mark_same(spread_ref, slice(c * BLOCK, rows), ids_ref[:, part(c)])
+    x_buf[...] = events_ref[...] * jnp.bfloat16(0.5)
+    pos = lax.axis_index("hist") * rows + lax.broadcasted_iota(jnp.int32, (rows, 1), 0)
 
     def emit(at, y):
-        if at < 3 * width:
-            put_heads(q_ref, at - 2 * width, y * (0.5 / math.sqrt(hd)), hd)
+        kind, at = at // width, at % width
+        if kind == 0:
+            gate_ref[:, at : at + y.shape[1]] = y
+        elif kind == 1:
+            put_heads(v_ref, at, jnp.where(pos < length_ref[0], y, 0.0), hd)
+        elif kind == 2:
+            put_heads(q_ref, at, y * (0.5 / math.sqrt(hd)), hd)
         else:
-            put_heads(k_buf, at - 3 * width, y, hd)
-
-    columns(x_ref, w_ref, 2 * width, 2 * width, emit)
+            put_heads(k_buf, at, y, hd)
+
+    columns(x_buf, w_ref, 0, 4 * width, emit)
     for h in range(heads):
         for c in range(blocks):
             rs = slice(c * BLOCK, rows)
@@ -255,29 +249,25 @@
     cut = rows // 2
     bf16 = functools.partial(jax.ShapeDtypeStruct, dtype=jnp.bfloat16)
     f32 = functools.partial(jax.ShapeDtypeStruct, dtype=jnp.float32)
-    stay = [pltpu.with_memory_space_constraint(a, pltpu.MemorySpace.HBM) for a in (events, w_proj, item_ids)]
-    high, low, x, gate, v, spread, own = kernel_call(
-        start_kernel,
-        (
-            bf16((cut + 16, width)), bf16((cut + 16, width)), bf16((rows, width)), f32((rows, width)),
-            bf16((heads, rows, hd)), jax.ShapeDtypeStruct((rows, 128), jnp.int32), bf16((rows, width)),
-        ),
-        [HBM] * 3 + [SMEM],
-        [
-            pltpu.VMEM((width, 2 * width), jnp.bfloat16),
-            pltpu.VMEM(item_ids.shape, jnp.int32),
-            pltpu.SemaphoreType.DMA((3,)),
-        ],
-        (*stay, lengths), 1000,
+    stay = [pltpu.with_memory_space_constraint(a, pltpu.MemorySpace.HBM) for a in (events, item_ids)]
+    high, low, x = kernel_call(
+        send_kernel, (bf16((cut + 16, width)), bf16((cut + 16, width)), bf16((rows, width))), [HBM] * 2,
+        [pltpu.VMEM(item_ids.shape, jnp.int32), pltpu.SemaphoreType.DMA((3,))], stay, 4000,
     )
     high = shifted(high, "hist", 1)
     low = shifted(low, "hist", 1)
-    q, mixed = kernel_call(
+    gate, _, spread, q, mixed = kernel_call(
         own_kernel,
-        (bf16((heads, rows, hd)), f32((heads, rows, hd))),
-        [SMEM] + [VMEM] * 5,
-        [pltpu.VMEM((heads, rows, hd), jnp.bfloat16), pltpu.VMEM((rows, rows), jnp.float32)],
-        (repeat_bias, x, w_proj, item_ids, spread, v), 6000,
+        (
+            f32((rows, width)), bf16((heads, rows, hd)), jax.ShapeDtypeStruct((rows, 128), jnp.int32),
+            bf16((heads, rows, hd)), f32((heads, rows, hd)),
+        ),
+        [SMEM] * 2 + [VMEM] * 3,
+        [
+            pltpu.VMEM((rows, width), jnp.bfloat16), pltpu.VMEM((heads, rows, hd), jnp.bfloat16),
+            pltpu.VMEM((rows, rows), jnp.float32),
+        ],
+        (lengths, repeat_bias, x, w_proj, item_ids), 7000,
     )
     piece = [
         pltpu.VMEM((cut, width), jnp.bfloat16),
@@ -289,7 +279,7 @@
         (f32((heads, rows, hd)), f32((2, 8, width))),
         [SMEM] * 2 + [VMEM] * 7,
         piece + [pltpu.VMEM((rows, cut), jnp.float32), pltpu.VMEM((cut, width), jnp.bfloat16)],
-        (lengths, repeat_bias, high, w_proj, spread, q, mixed, gate, own), 4000,
+        (lengths, repeat_bias, high, w_proj, spread, q, mixed, gate, x), 4000,
     )
     return kernel_call(
         low_kernel,

time: 102 us -> 99.8 us (0.978)
  waiting for transfers between devices: 5.38 us -> 3.5 us
    ppermute x2, waiting for transfers between devices: 5.38 us -> 3.5 us  [shifted(): return lax.ppermute(block, axis, route)]
  transfers between devices with their start and end apart: 2 -> 2, of which waited for: 1 -> 1; matrix products, arithmetic and copies ran while one was open for 0% -> 0% of each run, Pallas kernels for 9% -> 11%
where the time goes in v5:
time: 99.8 us; the launch traced here: 99.6 us
  blocking collectives  70.1 us (70%)
  Pallas kernels  17.3 us (17%)
  starting transfers between devices  7.95 us (8%)
  waiting for transfers between devices  3.5 us (4%)
    all_to_all x4, blocking collectives, swapped(): return lax.all_to_all(x, axis, 0, 0, tiled=True)  70.1 us
    pallas_call x4, Pallas kernels, kernel_call(): pl.pallas_call(kernel, out_shape=outs, in_specs=specs, out_specs=jax.tree...  15.5 us
    ppermute x2, starting transfers between devices, shifted(): return lax.ppermute(block, axis, route)  7.95 us
    ppermute x2, waiting for transfers between devices, shifted(): return lax.ppermute(block, axis, route)  3.5 us
  transfers between devices with their start and end apart: 2, of which 1 were waited for; matrix products, arithmetic and copies ran while one was open for 0% of the time, Pallas kernels for 11%

profile of v5, /device:TPU:1, one launch (start us, length us, event | category | flops | bytes accessed | tf_op | source)
XLA Modules:
  0.0 99.6 jit_solution(5711479356142314850)
XLA Ops:
  0.0 0.0 copy-start.4
  0.0 0.0 copy-start.3
  0.0 0.0 copy-start
  0.0 1.4 %shard_map.73 = (bf16[528,512]{1,0:T(8,128)(2,1)S(1)}, bf16[528,512]{1,0:T(8,128)(2,1)S(1)}, bf16[1024,512]{1,0:T(8,128)(2,1)S(1)}) custom-call(bf16[1,1024,512]{2,1,0:T(8,128)(2,1)} %x_hbm.1, s32[1,1024]{1,0:T(1,128)} %ids_ref.1), custom_call_target="tpu_custom_call" | custom-call | flops 4000000000 | bytes 10000000 | tf_op jit(solution)/shard_map/pallas_call | solution.py:234
  1.4 6.0 %collective-permute-start = (bf16[528,512]{1,0:T(8,128)(2,1)S(1)}, bf16[528,512]{1,0:T(8,128)(2,1)S(1)}, u32[]{:S(2)}, u32[]{:S(2)}) collective-permute-start(bf16[528,512]{1,0:T(8,128)(2,1)S(1)} %get-tuple-element.16), channel_id=1, source_target_pairs={{0,32},{32,64},{64,96},{96,128},{128,160},{160,192},{192,224},{224... | collective-permute-start | bytes 1622024 | tf_op jit(solution)/shard_map/ppermute | solution.py:227
  7.5 1.9 %collective-permute-start.1 = (bf16[528,512]{1,0:T(8,128)(2,1)S(1)}, bf16[528,512]{1,0:T(8,128)(2,1)S(1)}, u32[]{:S(2)}, u32[]{:S(2)}) collective-permute-start(bf16[528,512]{1,0:T(8,128)(2,1)S(1)} %get-tuple-element.20), channel_id=1, source_target_pairs={{0,32},{32,64},{64,96},{96,128},{128,160},{160,192},{192,224},{224... | collective-permute-start | bytes 1622024 | tf_op jit(solution)/shard_map/ppermute | solution.py:227
  10.0 0.0 copy-done.4
  10.1 0.0 copy-done.3
  10.1 0.0 copy-done
  10.1 6.0 %shard_map.74 = (f32[1024,512]{1,0:T(8,128)S(1)}, bf16[4,1024,128]{2,1,0:T(8,128)(2,1)}, s32[1024,128]{1,0:T(8,128)S(1)}, bf16[4,1024,128]{2,1,0:T(8,128)(2,1)S(1)}, f32[4,1024,128]{2,1,0:T(8,128)S(1)}) custom-call(s32[1]{0:T(128)S(6)} %copy.8.length_ref, f32[4]{0:T(128)S(1)} %copy-done.3, bf16[1024,512]{1,0:T(8,128)(2,1)S(1)} %get-tuple-element.17.events_ref, ...), custom_call_target="tpu_custom_call" | custom-call | flops 7000000000 | bytes 10000000 | tf_op jit(solution)/shard_map/pallas_call | solution.py:234
  16.0 3.5 %collective-permute-done.1.got_ref = bf16[528,512]{1,0:T(8,128)(2,1)S(1)} collective-permute-done((bf16[528,512]{1,0:T(8,128)(2,1)S(1)}, bf16[528,512]{1,0:T(8,128)(2,1)S(1)}, u32[]{:S(2)}, u32[]{:S(2)}) %collective-permute-start.1) | collective-permute-done | bytes 540704 | tf_op jit(solution)/shard_map/ppermute | solution.py:227
  19.5 0.0 copy-start.2
  19.5 4.6 %shard_map.75 = (f32[4,1024,128]{2,1,0:T(8,128)S(1)}, f32[2,8,512]{2,1,0:T(8,128)S(1)}) custom-call(s32[1]{0:T(128)S(6)} %copy.8.length_ref, f32[4]{0:T(128)S(1)} %copy-done.3, bf16[528,512]{1,0:T(8,128)(2,1)S(1)} %collective-permute-done.1.got_ref, bf16[512,2048]{1,0:T(8,128)(2,1)S(1)} %copy-done, s32[1024,128]{1,0:T(8,128)S(1)} %get-tuple-element.18.spread_ref, ...), custom_call_target="tpu_custom_call" | custom-call | flops 4000000000 | bytes 10000000 | tf_op jit(solution)/shard_map/pallas_call | solution.py:234
  24.2 0.0 collective-permute-done.got_ref
  24.2 0.0 copy-done.2
  24.2 0.0 copy-start.1
  24.2 3.5 %shard_map.76 = f32[16,1,512]{2,1,0:T(1,128)S(1)} custom-call(s32[1]{0:T(128)S(6)} %copy.8.length_ref, f32[4]{0:T(128)S(1)} %copy-done.3, bf16[528,512]{1,0:T(8,128)(2,1)S(1)} %collective-permute-done.got_ref, bf16[512,2048]{1,0:T(8,128)(2,1)S(1)} %copy-done, s32[1024,128]{1,0:T(8,128)S(1)} %get-tuple-element.18.spread_ref, ...), custom_call_target="tpu_custom_call" | custom-call | flops 2000000000 | bytes 10000000 | tf_op jit(solution)/shard_map/pallas_call | solution.py:234
  27.7 15.4 %all_to_all.20.parts_ref = f32[16,1,512]{2,1,0:T(1,128)S(1)} all-to-all(f32[16,1,512]{2,1,0:T(1,128)S(1)} %shard_map.76), channel_id=1, replica_groups=mesh['hist'=16,'item'=32] {'hist'}, dimensions={0} | all-to-all | bytes 65536 | tf_op jit(solution)/shard_map/all_to_all | solution.py:354
  43.1 0.1 shard_map.77
  43.3 27.6 %all_to_all.21.vecs_ref = f32[32,1,512]{2,1,0:T(1,128)S(1)} all-to-all(f32[32,1,512]{2,1,0:T(1,128)S(1)} %shard_map.77), channel_id=1, replica_groups=mesh['hist'=16,'item'=32] {'item'}, dimensions={0} | all-to-all | bytes 131072 | tf_op jit(solution)/shard_map/all_to_all | solution.py:354
  70.9 0.0 copy-done.1
  70.9 0.7 shard_map.78
  71.5 12.0 %all_to_all.22.parts_ref = f32[16,1,128]{2,1,0:T(1,128)S(1)} all-to-all(f32[16,1,128]{2,1,0:T(1,128)S(1)} %get-tuple-element.25), channel_id=1, replica_groups=mesh['hist'=16,'item'=32] {'hist'}, dimensions={0} | all-to-all | bytes 16384 | tf_op jit(solution)/shard_map/all_to_all | solution.py:354
  83.5 0.1 shard_map.79
  83.6 15.1 %all_to_all.23.parts_ref = f32[32,1,128]{2,1,0:T(1,128)S(1)} all-to-all(f32[32,1,128]{2,1,0:T(1,128)S(1)} %shard_map.79), channel_id=1, replica_groups=mesh['hist'=16,'item'=32] {'item'}, dimensions={0} | all-to-all | bytes 32768 | tf_op jit(solution)/shard_map/all_to_all | solution.py:354
  98.7 0.9 shard_map.80
Async XLA Ops:
  0.0 10.0 %copy-start.4 = (s32[1,1024]{1,0:T(1,128)S(1)}, s32[1,1024]{1,0:T(1,128)}, u32[]{:S(2)}) copy-start(s32[1,1024]{1,0:T(1,128)} %ids_ref.1) | copy-start | bytes 12292
  0.0 10.1 %copy-start.3 = (f32[4]{0:T(128)S(1)}, f32[4]{0:T(128)}, u32[]{:S(2)}) copy-start(f32[4]{0:T(128)} %bias_ref.5) | copy-start | bytes 52
  0.0 10.1 %copy-start = (bf16[512,2048]{1,0:T(8,128)(2,1)S(1)}, bf16[512,2048]{1,0:T(8,128)(2,1)}, u32[]{:S(2)}) copy-start(bf16[512,2048]{1,0:T(8,128)(2,1)} %w_ref.5) | copy-start | bytes 6291460
  1.4 22.7 %collective-permute-start = (bf16[528,512]{1,0:T(8,128)(2,1)S(1)}, bf16[528,512]{1,0:T(8,128)(2,1)S(1)}, u32[]{:S(2)}, u32[]{:S(2)}) collective-permute-start(bf16[528,512]{1,0:T(8,128)(2,1)S(1)} %get-tuple-element.16), channel_id=1, source_target_pairs={{0,32},{32,64},{64,96},{96,128},{128,160},{160,192},{192,224},{224... | collective-permute-start | bytes 1622024 | tf_op jit(solution)/shard_map/ppermute | solution.py:227
  7.5 12.1 %collective-permute-start.1 = (bf16[528,512]{1,0:T(8,128)(2,1)S(1)}, bf16[528,512]{1,0:T(8,128)(2,1)S(1)}, u32[]{:S(2)}, u32[]{:S(2)}) collective-permute-start(bf16[528,512]{1,0:T(8,128)(2,1)S(1)} %get-tuple-element.20), channel_id=1, source_target_pairs={{0,32},{32,64},{64,96},{96,128},{128,160},{160,192},{192,224},{224... | collective-permute-start | bytes 1622024 | tf_op jit(solution)/shard_map/ppermute | solution.py:227
  19.5 4.6 %copy-start.2 = (bf16[512,512]{1,0:T(8,128)(2,1)S(1)}, bf16[512,512]{1,0:T(8,128)(2,1)}, u32[]{:S(2)}) copy-start(bf16[512,512]{1,0:T(8,128)(2,1)} %w_out_ref.1) | copy-start | bytes 1572868
  24.2 46.7 %copy-start.1 = (bf16[1024,512]{1,0:T(8,128)(2,1)S(1)}, bf16[1024,512]{1,0:T(8,128)(2,1)}, u32[]{:S(2)}) copy-start(bf16[1024,512]{1,0:T(8,128)(2,1)} %slab_ref.1) | copy-start | bytes 3145732

commit v6 on v5

--- a/solution.py
+++ b/solution.py
@@ -69,27 +69,21 @@
     return (rows[0:1] + 128.0 * rows[1:2] + 16384.0 * rows[2:3]).astype(jnp.int32)
 
 
-def send_kernel(x_hbm, ids_hbm, high_ref, low_ref, events_ref, ids_ref, sems):
+def send_kernel(first, x_hbm, ids_hbm, out_ref, ids_ref, sems):
     cut = ids_ref.shape[1] // 2
     copies = [
-        pltpu.make_async_copy(x_hbm.at[0, cut:], events_ref.at[cut:], sems.at[0]),
-        pltpu.make_async_copy(x_hbm.at[0, :cut], events_ref.at[:cut], sems.at[1]),
-        pltpu.make_async_copy(ids_hbm, ids_ref, sems.at[2]),
+        pltpu.make_async_copy(x_hbm.at[0, first : first + cut], out_ref.at[:cut], sems.at[0]),
+        pltpu.make_async_copy(ids_hbm, ids_ref, sems.at[1]),
     ]
     for copy in copies:
         copy.start()
-    copies[2].wait()
-    ids = ids_ref[...]
-    high_ref[cut:, :] = digit_rows(ids[:, cut:])
-    low_ref[cut:, :] = digit_rows(ids[:, :cut])
+    copies[1].wait()
+    out_ref[cut:, :] = digit_rows(ids_ref[:, first : first + cut])
     copies[0].wait()
-    high_ref[:cut, :] = events_ref[cut:, :]
-    copies[1].wait()
-    low_ref[:cut, :] = events_ref[:cut, :]
 
 
 def own_kernel(
-    length_ref, bias_ref, events_ref, w_ref, ids_ref, gate_ref, v_ref, spread_ref, q_ref, part_ref,
+    length_ref, bias_ref, high_ref, low_ref, w_ref, ids_ref, gate_ref, v_ref, spread_ref, q_ref, part_ref,
     x_buf, k_buf, same_buf,
 ):
     rows, width = x_buf.shape
@@ -99,7 +93,9 @@
     spread_ids(ids_ref[...], spread_ref)
     for c in range(blocks):
         same_buf[c * BLOCK :, part(c)] = mark_same(spread_ref, slice(c * BLOCK, rows), ids_ref[:, part(c)])
-    x_buf[...] = events_ref[...] * jnp.bfloat16(0.5)
+    cut = rows // 2
+    x_buf[:cut, :] = low_ref[:cut, :] * jnp.bfloat16(0.5)
+    x_buf[cut:, :] = high_ref[:cut, :] * jnp.bfloat16(0.5)
     pos = lax.axis_index("hist") * rows + lax.broadcasted_iota(jnp.int32, (rows, 1), 0)
 
     def emit(at, y):
@@ -107,7 +103,7 @@
         if kind == 0:
             gate_ref[:, at : at + y.shape[1]] = y
         elif kind == 1:
-            put_heads(v_ref, at, jnp.where(pos < length_ref[0], y, 0.0), hd)
+            put_heads(v_ref, at, jnp.where(pos < length_ref[:1, :1], y, 0.0), hd)
         elif kind == 2:
             put_heads(q_ref, at, y * (0.5 / math.sqrt(hd)), hd)
         else:
@@ -158,9 +154,8 @@
     heads, _, hd = mix_ref.shape
     width = heads * hd
 
-    def norm_rows(b, carry):
-        at = pl.multiple_of(b * NORM_ROWS, NORM_ROWS)
-        rs = pl.ds(first + at, NORM_ROWS)
+    for at in range(0, rows, NORM_ROWS):
+        rs = slice(first + at, first + at + NORM_ROWS)
         mixed = [mix_ref[h, rs, :] for h in range(heads)]
         mean = jnp.sum(sum(mixed), axis=1, keepdims=True) * (1.0 / width)
         mixed = [m - mean for m in mixed]
@@ -168,10 +163,7 @@
         factor = lax.rsqrt(spread + 1e-06 * WINDOW * WINDOW)
         for h in range(heads):
             gated = mixed[h] * factor * gate_ref[rs, h * hd : (h + 1) * hd]
-            gated_buf[pl.ds(at, NORM_ROWS), h * hd : (h + 1) * hd] = gated.astype(jnp.bfloat16)
-        return carry
-
-    lax.fori_loop(0, rows // NORM_ROWS, norm_rows, 0, unroll=NORM_UNROLL)
+            gated_buf[at : at + NORM_ROWS, h * hd : (h + 1) * hd] = gated.astype(jnp.bfloat16)
     return mm(valid(first, rows, length), gated_buf[...])
 
 
@@ -181,17 +173,17 @@
 
 
 def high_kernel(
-    length_ref, bias_ref, got_ref, w_ref, spread_ref, q_ref, part_ref, gate_ref, events_ref,
+    length_ref, bias_ref, got_ref, w_ref, spread_ref, q_ref, part_ref, gate_ref, high_ref, low_ref,
     mix_ref, sums_ref, x_buf, k_buf, v_buf, same_buf, gated_buf,
 ):
     rows = q_ref.shape[1]
     cut = rows // 2
-    length = length_ref[0]
+    length = length_ref[:1, :1]
     halo_piece(
         cut // BLOCK, length, bias_ref, got_ref, w_ref, spread_ref, q_ref, part_ref, x_buf, k_buf, v_buf, same_buf, mix_ref
     )
     sums_ref[0] = gated_sum(cut, rows - cut, length, mix_ref, gate_ref, gated_buf)
-    sums_ref[1] = mm(valid(0, rows, length), events_ref[...])
+    sums_ref[1] = mm(valid(0, cut, length), low_ref[:cut, :]) + mm(valid(cut, cut, length), high_ref[:cut, :])
 
 
 def low_kernel(
@@ -199,7 +191,7 @@
     out_ref, x_buf, k_buf, v_buf, same_buf, mix_buf, gated_buf,
 ):
     cut = gated_buf.shape[0]
-    length = length_ref[0]
+    length = length_ref[:1, :1]
     halo_piece(0, length, bias_ref, got_ref, w_ref, spread_ref, q_ref, part_ref, x_buf, k_buf, v_buf, same_buf, mix_buf)
     total = sums_ref[0] + gated_sum(0, cut, length, mix_buf, gate_ref, gated_buf)
     high = total.astype(jnp.bfloat16).astype(jnp.float32)
@@ -214,7 +206,6 @@
 
 
 NORM_ROWS = 32
-NORM_UNROLL = 4
 
 
 SMEM = pl.BlockSpec(memory_space=pltpu.SMEM)
@@ -250,24 +241,30 @@
     bf16 = functools.partial(jax.ShapeDtypeStruct, dtype=jnp.bfloat16)
     f32 = functools.partial(jax.ShapeDtypeStruct, dtype=jnp.float32)
     stay = [pltpu.with_memory_space_constraint(a, pltpu.MemorySpace.HBM) for a in (events, item_ids)]
-    high, low, x = kernel_call(
-        send_kernel, (bf16((cut + 16, width)), bf16((cut + 16, width)), bf16((rows, width))), [HBM] * 2,
-        [pltpu.VMEM(item_ids.shape, jnp.int32), pltpu.SemaphoreType.DMA((3,))], stay, 4000,
-    )
-    high = shifted(high, "hist", 1)
-    low = shifted(low, "hist", 1)
+
+    def send(first, mflops):
+        return kernel_call(
+            functools.partial(send_kernel, first), bf16((cut + 16, width)), [HBM] * 2,
+            [pltpu.VMEM(item_ids.shape, jnp.int32), pltpu.SemaphoreType.DMA((2,))], stay, mflops,
+        )
+
+    length = jnp.broadcast_to(lengths[:, None], (8, 128))
+    own_high = send(cut, 2000)
+    high = shifted(own_high, "hist", 1)
+    own_low = send(0, 2000)
+    low = shifted(own_low, "hist", 1)
     gate, _, spread, q, mixed = kernel_call(
         own_kernel,
         (
             f32((rows, width)), bf16((heads, rows, hd)), jax.ShapeDtypeStruct((rows, 128), jnp.int32),
             bf16((heads, rows, hd)), f32((heads, rows, hd)),
         ),
-        [SMEM] * 2 + [VMEM] * 3,
+        [VMEM, SMEM] + [VMEM] * 4,
         [
             pltpu.VMEM((rows, width), jnp.bfloat16), pltpu.VMEM((heads, rows, hd), jnp.bfloat16),
             pltpu.VMEM((rows, rows), jnp.float32),
         ],
-        (lengths, repeat_bias, x, w_proj, item_ids), 7000,
+        (length, repeat_bias, own_high, own_low, w_proj, item_ids), 7000,
     )
     piece = [
         pltpu.VMEM((cut, width), jnp.bfloat16),
@@ -277,19 +274,19 @@
     mixed, sums = kernel_call(
         high_kernel,
         (f32((heads, rows, hd)), f32((2, 8, width))),
-        [SMEM] * 2 + [VMEM] * 7,
+        [VMEM, SMEM] + [VMEM] * 8,
         piece + [pltpu.VMEM((rows, cut), jnp.float32), pltpu.VMEM((cut, width), jnp.bfloat16)],
-        (lengths, repeat_bias, high, w_proj, spread, q, mixed, gate, x), 4000,
+        (length, repeat_bias, high, w_proj, spread, q, mixed, gate, own_high, own_low), 4000,
     )
     return kernel_call(
         low_kernel,
         f32((lax.axis_size("hist"), 1, width)),
-        [SMEM] * 2 + [VMEM] * 8,
+        [VMEM, SMEM] + [VMEM] * 8,
         piece + [
             pltpu.VMEM((cut, cut), jnp.float32), pltpu.VMEM((heads, cut, hd), jnp.float32),
             pltpu.VMEM((cut, width), jnp.bfloat16),
         ],
-        (lengths, repeat_bias, low, w_proj, spread, q, mixed, gate, sums, w_out), 2000,
+        (length, repeat_bias, low, w_proj, spread, q, mixed, gate, sums, w_out), 2000,
     )
 
 

time: 99.8 us -> 94.4 us (0.946)
  waiting for transfers between devices: 3.5 us -> 0.01 us
  blocking collectives: 70.1 us -> 68.3 us
    ppermute x2, waiting for transfers between devices: 3.5 us -> 0.01 us  [shifted(): return lax.ppermute(block, axis, route)]
    all_to_all x4, blocking collectives: 70.1 us -> 68.3 us  [swapped(): return lax.all_to_all(x, axis, 0, 0, tiled=True)]
    pallas_call x4 -> x5, Pallas kernels: 15.5 us -> 15.1 us  [kernel_call(): pl.pallas_call(kernel, out_shape=outs, in_specs=specs, out_specs=jax.tree...]
  transfers between devices with their start and end apart: 2 -> 2, of which waited for: 1 -> 0; matrix products, arithmetic and copies ran while one was open for 0% -> 0% of each run, Pallas kernels for 11% -> 12%
where the time goes in v6:
time: 94.4 us; the launch traced here: 94.1 us
  blocking collectives  68.3 us (72%)
  Pallas kernels  16.9 us (18%)
  starting transfers between devices  8.08 us (9%)
    all_to_all x4, blocking collectives, swapped(): return lax.all_to_all(x, axis, 0, 0, tiled=True)  68.3 us
    pallas_call x5, Pallas kernels, kernel_call(): pl.pallas_call(kernel, out_shape=outs, in_specs=specs, out_specs=jax.tree...  15.1 us
    ppermute x2, starting transfers between devices, shifted(): return lax.ppermute(block, axis, route)  8.08 us
  transfers between devices with their start and end apart: 2, of which 0 were waited for; matrix products, arithmetic and copies ran while one was open for 0% of the time, Pallas kernels for 12%

profile of v6, /device:TPU:1, one launch (start us, length us, event | category | flops | bytes accessed | tf_op | source)
XLA Modules:
  0.0 94.1 jit_solution(1435082649956483000)
XLA Ops:
  0.0 1.1 %shard_map.74.high_ref = bf16[528,512]{1,0:T(8,128)(2,1)S(1)} custom-call(bf16[1,1024,512]{2,1,0:T(8,128)(2,1)} %x_hbm.3, s32[1,1024]{1,0:T(1,128)} %ids_ref.1), custom_call_target="tpu_custom_call" | custom-call | flops 2000000000 | bytes 10000000 | tf_op jit(solution)/shard_map/pallas_call | solution.py:225
  1.1 0.0 copy-start
  1.1 0.0 copy-start.3
  1.1 0.0 copy-start.4
  1.1 6.2 %collective-permute-start.1 = (bf16[528,512]{1,0:T(8,128)(2,1)S(1)}, bf16[528,512]{1,0:T(8,128)(2,1)S(1)}, u32[]{:S(2)}, u32[]{:S(2)}) collective-permute-start(bf16[528,512]{1,0:T(8,128)(2,1)S(1)} %shard_map.74.high_ref), channel_id=1, source_target_pairs={{0,32},{32,64},{64,96},{96,128},{128,160},{160,192},{192,224},{224... | collective-permute-start | bytes 1622024 | tf_op jit(solution)/shard_map/ppermute | solution.py:218
  7.3 1.1 %shard_map.73.low_ref = bf16[528,512]{1,0:T(8,128)(2,1)S(1)} custom-call(bf16[1,1024,512]{2,1,0:T(8,128)(2,1)} %x_hbm.3, s32[1,1024]{1,0:T(1,128)} %ids_ref.1), custom_call_target="tpu_custom_call" | custom-call | flops 2000000000 | bytes 10000000 | tf_op jit(solution)/shard_map/pallas_call | solution.py:225
  8.3 1.9 %collective-permute-start = (bf16[528,512]{1,0:T(8,128)(2,1)S(1)}, bf16[528,512]{1,0:T(8,128)(2,1)S(1)}, u32[]{:S(2)}, u32[]{:S(2)}) collective-permute-start(bf16[528,512]{1,0:T(8,128)(2,1)S(1)} %shard_map.73.low_ref), channel_id=1, source_target_pairs={{0,32},{32,64},{64,96},{96,128},{128,160},{160,192},{192,224},{224... | collective-permute-start | bytes 1622024 | tf_op jit(solution)/shard_map/ppermute | solution.py:218
  10.9 0.0 copy-done
  10.9 0.0 copy-done.3
  10.9 0.0 copy-done.4
  11.0 6.0 %shard_map.75 = (f32[1024,512]{1,0:T(8,128)S(1)}, bf16[4,1024,128]{2,1,0:T(8,128)(2,1)}, s32[1024,128]{1,0:T(8,128)S(1)}, bf16[4,1024,128]{2,1,0:T(8,128)(2,1)S(1)}, f32[4,1024,128]{2,1,0:T(8,128)S(1)}) custom-call(s32[8,128]{1,0:T(8,128)S(1)} %broadcast_in_dim.9.length_ref, f32[4]{0:T(128)S(1)} %copy-done.3, bf16[528,512]{1,0:T(8,128)(2,1)S(1)} %shard_map.74.high_ref, ...), custom_call_target="tpu_custom_call" | custom-call | flops 7000000000 | bytes 10000000 | tf_op jit(solution)/shard_map/pallas_call | solution.py:225
  16.9 0.0 collective-permute-done.1.got_ref
  16.9 0.0 copy-start.2
  17.0 4.1 %shard_map.76 = (f32[4,1024,128]{2,1,0:T(8,128)S(1)}, f32[2,8,512]{2,1,0:T(8,128)S(1)}) custom-call(s32[8,128]{1,0:T(8,128)S(1)} %broadcast_in_dim.9.length_ref, f32[4]{0:T(128)S(1)} %copy-done.3, bf16[528,512]{1,0:T(8,128)(2,1)S(1)} %collective-permute-done.1.got_ref, bf16[512,2048]{1,0:T(8,128)(2,1)S(1)} %copy-done, ...), custom_call_target="tpu_custom_call" | custom-call | flops 4000000000 | bytes 10000000 | tf_op jit(solution)/shard_map/pallas_call | solution.py:225
  21.1 0.0 collective-permute-done.got_ref
  21.1 0.0 copy-done.2
  21.1 0.0 copy-start.1
  21.1 3.0 %shard_map.77 = f32[16,1,512]{2,1,0:T(1,128)S(1)} custom-call(s32[8,128]{1,0:T(8,128)S(1)} %broadcast_in_dim.9.length_ref, f32[4]{0:T(128)S(1)} %copy-done.3, bf16[528,512]{1,0:T(8,128)(2,1)S(1)} %collective-permute-done.got_ref, bf16[512,2048]{1,0:T(8,128)(2,1)S(1)} %copy-done, s32[1024,128]{1,0:T(8,128)S(1)} %get-tuple-element.13.spread_ref, ...), custom_call_target="tpu_custom_call" | custom-call | flops 2000000000 | bytes 10000000 | tf_op jit(solution)/shard_map/pallas_call | solution.py:225
  24.0 13.7 %all_to_all.20.parts_ref = f32[16,1,512]{2,1,0:T(1,128)S(1)} all-to-all(f32[16,1,512]{2,1,0:T(1,128)S(1)} %shard_map.77), channel_id=1, replica_groups=mesh['hist'=16,'item'=32] {'hist'}, dimensions={0} | all-to-all | bytes 65536 | tf_op jit(solution)/shard_map/all_to_all | solution.py:351
  37.7 0.1 shard_map.78
  37.8 27.6 %all_to_all.21.vecs_ref = f32[32,1,512]{2,1,0:T(1,128)S(1)} all-to-all(f32[32,1,512]{2,1,0:T(1,128)S(1)} %shard_map.78), channel_id=1, replica_groups=mesh['hist'=16,'item'=32] {'item'}, dimensions={0} | all-to-all | bytes 131072 | tf_op jit(solution)/shard_map/all_to_all | solution.py:351
  65.4 0.0 copy-done.1
  65.4 0.7 shard_map.79
  66.1 12.0 %all_to_all.22.parts_ref = f32[16,1,128]{2,1,0:T(1,128)S(1)} all-to-all(f32[16,1,128]{2,1,0:T(1,128)S(1)} %get-tuple-element.19), channel_id=1, replica_groups=mesh['hist'=16,'item'=32] {'hist'}, dimensions={0} | all-to-all | bytes 16384 | tf_op jit(solution)/shard_map/all_to_all | solution.py:351
  78.1 0.1 shard_map.80
  78.2 15.1 %all_to_all.23.parts_ref = f32[32,1,128]{2,1,0:T(1,128)S(1)} all-to-all(f32[32,1,128]{2,1,0:T(1,128)S(1)} %shard_map.80), channel_id=1, replica_groups=mesh['hist'=16,'item'=32] {'item'}, dimensions={0} | all-to-all | bytes 32768 | tf_op jit(solution)/shard_map/all_to_all | solution.py:351
  93.2 0.9 shard_map.81
  (1 shorter events, 0.0 us)
Async XLA Ops:
  1.1 9.9 %copy-start = (bf16[512,2048]{1,0:T(8,128)(2,1)S(1)}, bf16[512,2048]{1,0:T(8,128)(2,1)}, u32[]{:S(2)}) copy-start(bf16[512,2048]{1,0:T(8,128)(2,1)} %w_ref.5) | copy-start | bytes 6291460
  1.1 9.9 %copy-start.3 = (f32[4]{0:T(128)S(1)}, f32[4]{0:T(128)}, u32[]{:S(2)}) copy-start(f32[4]{0:T(128)} %bias_ref.5) | copy-start | bytes 52
  1.1 9.9 %copy-start.4 = (s32[1,1024]{1,0:T(1,128)S(1)}, s32[1,1024]{1,0:T(1,128)}, u32[]{:S(2)}) copy-start(s32[1,1024]{1,0:T(1,128)} %ids_ref.1) | copy-start | bytes 12292
  1.1 15.8 %collective-permute-start.1 = (bf16[528,512]{1,0:T(8,128)(2,1)S(1)}, bf16[528,512]{1,0:T(8,128)(2,1)S(1)}, u32[]{:S(2)}, u32[]{:S(2)}) collective-permute-start(bf16[528,512]{1,0:T(8,128)(2,1)S(1)} %shard_map.74.high_ref), channel_id=1, source_target_pairs={{0,32},{32,64},{64,96},{96,128},{128,160},{160,192},{192,224},{224... | collective-permute-start | bytes 1622024 | tf_op jit(solution)/shard_map/ppermute | solution.py:218
  8.3 12.7 %collective-permute-start = (bf16[528,512]{1,0:T(8,128)(2,1)S(1)}, bf16[528,512]{1,0:T(8,128)(2,1)S(1)}, u32[]{:S(2)}, u32[]{:S(2)}) collective-permute-start(bf16[528,512]{1,0:T(8,128)(2,1)S(1)} %shard_map.73.low_ref), channel_id=1, source_target_pairs={{0,32},{32,64},{64,96},{96,128},{128,160},{160,192},{192,224},{224... | collective-permute-start | bytes 1622024 | tf_op jit(solution)/shard_map/ppermute | solution.py:218
  16.9 4.1 %copy-start.2 = (bf16[512,512]{1,0:T(8,128)(2,1)S(1)}, bf16[512,512]{1,0:T(8,128)(2,1)}, u32[]{:S(2)}) copy-start(bf16[512,512]{1,0:T(8,128)(2,1)} %w_out_ref.1) | copy-start | bytes 1572868
  21.1 44.4 %copy-start.1 = (bf16[1024,512]{1,0:T(8,128)(2,1)S(1)}, bf16[1024,512]{1,0:T(8,128)(2,1)}, u32[]{:S(2)}) copy-start(bf16[1024,512]{1,0:T(8,128)(2,1)} %slab_ref.1) | copy-start | bytes 3145732

commit v7 on v6

--- a/solution.py
+++ b/solution.py
@@ -30,6 +30,11 @@
 def mark_same(spread, rows, ids):
     mine = jnp.concatenate([spread[rows, :]] * (ids.shape[1] // 128), axis=1)
     return jnp.where(mine == ids, 1.0, 0.0)
+
+
+def spread_length(length_ref, rows, lanes):
+    tile = jnp.concatenate([length_ref[...]] * (lanes // 128), axis=1)
+    return jnp.concatenate([tile] * (rows // 8), axis=0) if rows > 8 else tile
 
 
 def triangle(below):
@@ -96,14 +101,14 @@
     cut = rows // 2
     x_buf[:cut, :] = low_ref[:cut, :] * jnp.bfloat16(0.5)
     x_buf[cut:, :] = high_ref[:cut, :] * jnp.bfloat16(0.5)
-    pos = lax.axis_index("hist") * rows + lax.broadcasted_iota(jnp.int32, (rows, 1), 0)
+    pos = lax.axis_index("hist") * rows + lax.broadcasted_iota(jnp.int32, (rows, 256), 0)
 
     def emit(at, y):
         kind, at = at // width, at % width
         if kind == 0:
             gate_ref[:, at : at + y.shape[1]] = y
         elif kind == 1:
-            put_heads(v_ref, at, jnp.where(pos < length_ref[:1, :1], y, 0.0), hd)
+            put_heads(v_ref, at, jnp.where(pos < spread_length(length_ref, rows, 256), y, 0.0), hd)
         elif kind == 2:
             put_heads(q_ref, at, y * (0.5 / math.sqrt(hd)), hd)
         else:
@@ -120,7 +125,7 @@
             part_ref[h, rs, :] = term if c == 0 else part_ref[h, rs, :] + term
 
 
-def halo_piece(first, length, bias_ref, got_ref, w_ref, spread_ref, q_ref, part_ref, x_buf, k_buf, v_buf, same_buf, mix_ref):
+def halo_piece(first, length_ref, bias_ref, got_ref, w_ref, spread_ref, q_ref, part_ref, x_buf, k_buf, v_buf, same_buf, mix_ref):
     heads, _, hd = q_ref.shape
     keys, width = x_buf.shape
     blocks = keys // BLOCK
@@ -130,11 +135,11 @@
     for c in range(blocks):
         end = (first + c + 1) * BLOCK
         same_buf[:end, part(c)] = mark_same(spread_ref, slice(0, end), ids[:, part(c)])
-    pos = lax.axis_index("hist") * WINDOW - WINDOW + first * BLOCK + lax.broadcasted_iota(jnp.int32, (keys, 1), 0)
+    pos = lax.axis_index("hist") * WINDOW - WINDOW + first * BLOCK + lax.broadcasted_iota(jnp.int32, (keys, 256), 0)
 
     def emit(at, y):
         if at < 2 * width:
-            put_heads(v_buf, at - width, jnp.where((pos >= 0) & (pos < length), y, 0.0), hd)
+            put_heads(v_buf, at - width, jnp.where((pos >= 0) & (pos < spread_length(length_ref, keys, 256)), y, 0.0), hd)
         else:
             put_heads(k_buf, at - 3 * width, y, hd)
 
@@ -150,7 +155,7 @@
             mix_ref[h, rs, :] = (part_ref if c == blocks - 1 else mix_ref)[h, rs, :] + term
 
 
-def gated_sum(first, rows, length, mix_ref, gate_ref, gated_buf):
+def gated_sum(first, rows, length_ref, mix_ref, gate_ref, gated_buf):
     heads, _, hd = mix_ref.shape
     width = heads * hd
 
@@ -164,12 +169,12 @@
         for h in range(heads):
             gated = mixed[h] * factor * gate_ref[rs, h * hd : (h + 1) * hd]
             gated_buf[at : at + NORM_ROWS, h * hd : (h + 1) * hd] = gated.astype(jnp.bfloat16)
-    return mm(valid(first, rows, length), gated_buf[...])
-
-
-def valid(first, rows, length):
+    return mm(valid(first, rows, length_ref), gated_buf[...])
+
+
+def valid(first, rows, length_ref):
     place = lax.axis_index("hist") * WINDOW + first + lax.broadcasted_iota(jnp.int32, (8, rows), 1)
-    return jnp.where(place < length, 1.0, 0.0).astype(jnp.bfloat16)
+    return jnp.where(place < spread_length(length_ref, 8, rows), 1.0, 0.0).astype(jnp.bfloat16)
 
 
 def high_kernel(
@@ -178,12 +183,11 @@
 ):
     rows = q_ref.shape[1]
     cut = rows // 2
-    length = length_ref[:1, :1]
     halo_piece(
-        cut // BLOCK, length, bias_ref, got_ref, w_ref, spread_ref, q_ref, part_ref, x_buf, k_buf, v_buf, same_buf, mix_ref
-    )
-    sums_ref[0] = gated_sum(cut, rows - cut, length, mix_ref, gate_ref, gated_buf)
-    sums_ref[1] = mm(valid(0, cut, length), low_ref[:cut, :]) + mm(valid(cut, cut, length), high_ref[:cut, :])
+        cut // BLOCK, length_ref, bias_ref, got_ref, w_ref, spread_ref, q_ref, part_ref, x_buf, k_buf, v_buf, same_buf, mix_ref
+    )
+    sums_ref[0] = gated_sum(cut, rows - cut, length_ref, mix_ref, gate_ref, gated_buf)
+    sums_ref[1] = mm(valid(0, cut, length_ref), low_ref[:cut, :]) + mm(valid(cut, cut, length_ref), high_ref[:cut, :])
 
 
 def low_kernel(
@@ -191,9 +195,8 @@
     out_ref, x_buf, k_buf, v_buf, same_buf, mix_buf, gated_buf,
 ):
     cut = gated_buf.shape[0]
-    length = length_ref[:1, :1]
-    halo_piece(0, length, bias_ref, got_ref, w_ref, spread_ref, q_ref, part_ref, x_buf, k_buf, v_buf, same_buf, mix_buf)
-    total = sums_ref[0] + gated_sum(0, cut, length, mix_buf, gate_ref, gated_buf)
+    halo_piece(0, length_ref, bias_ref, got_ref, w_ref, spread_ref, q_ref, part_ref, x_buf, k_buf, v_buf, same_buf, mix_buf)
+    total = sums_ref[0] + gated_sum(0, cut, length_ref, mix_buf, gate_ref, gated_buf)
     high = total.astype(jnp.bfloat16).astype(jnp.float32)
     middle = (total - high).astype(jnp.bfloat16).astype(jnp.float32)
     low = total - high - middle

time: 94.4 us -> 94.5 us (level)
  no operation moved by 1% of the time
where the time goes in v7:
time: 94.5 us; the launch traced here: 94.1 us
  blocking collectives  68.3 us (72%)
  Pallas kernels  16.9 us (18%)
  starting transfers between devices  8.08 us (9%)
    all_to_all x4, blocking collectives, swapped(): return lax.all_to_all(x, axis, 0, 0, tiled=True)  68.3 us
    pallas_call x5, Pallas kernels, kernel_call(): pl.pallas_call(kernel, out_shape=outs, in_specs=specs, out_specs=jax.tree...  15.2 us
    ppermute x2, starting transfers between devices, shifted(): return lax.ppermute(block, axis, route)  8.08 us
  transfers between devices with their start and end apart: 2, of which 0 were waited for; matrix products, arithmetic and copies ran while one was open for 0% of the time, Pallas kernels for 12%

profile of v7, /device:TPU:1, one launch (start us, length us, event | category | flops | bytes accessed | tf_op | source)
XLA Modules:
  0.0 94.1 jit_solution(17824719400750529044)
XLA Ops:
  0.0 1.1 %shard_map.74.high_ref = bf16[528,512]{1,0:T(8,128)(2,1)S(1)} custom-call(bf16[1,1024,512]{2,1,0:T(8,128)(2,1)} %x_hbm.3, s32[1,1024]{1,0:T(1,128)} %ids_ref.1), custom_call_target="tpu_custom_call" | custom-call | flops 2000000000 | bytes 10000000 | tf_op jit(solution)/shard_map/pallas_call | solution.py:228
  1.1 0.0 copy-start
  1.1 0.0 copy-start.3
  1.1 0.0 copy-start.4
  1.1 6.2 %collective-permute-start.1 = (bf16[528,512]{1,0:T(8,128)(2,1)S(1)}, bf16[528,512]{1,0:T(8,128)(2,1)S(1)}, u32[]{:S(2)}, u32[]{:S(2)}) collective-permute-start(bf16[528,512]{1,0:T(8,128)(2,1)S(1)} %shard_map.74.high_ref), channel_id=1, source_target_pairs={{0,32},{32,64},{64,96},{96,128},{128,160},{160,192},{192,224},{224... | collective-permute-start | bytes 1622024 | tf_op jit(solution)/shard_map/ppermute | solution.py:221
  7.3 1.1 %shard_map.73.low_ref = bf16[528,512]{1,0:T(8,128)(2,1)S(1)} custom-call(bf16[1,1024,512]{2,1,0:T(8,128)(2,1)} %x_hbm.3, s32[1,1024]{1,0:T(1,128)} %ids_ref.1), custom_call_target="tpu_custom_call" | custom-call | flops 2000000000 | bytes 10000000 | tf_op jit(solution)/shard_map/pallas_call | solution.py:228
  8.3 1.9 %collective-permute-start = (bf16[528,512]{1,0:T(8,128)(2,1)S(1)}, bf16[528,512]{1,0:T(8,128)(2,1)S(1)}, u32[]{:S(2)}, u32[]{:S(2)}) collective-permute-start(bf16[528,512]{1,0:T(8,128)(2,1)S(1)} %shard_map.73.low_ref), channel_id=1, source_target_pairs={{0,32},{32,64},{64,96},{96,128},{128,160},{160,192},{192,224},{224... | collective-permute-start | bytes 1622024 | tf_op jit(solution)/shard_map/ppermute | solution.py:221
  10.9 0.0 copy-done
  10.9 0.0 copy-done.3
  10.9 0.0 copy-done.4
  11.0 6.0 %shard_map.75 = (f32[1024,512]{1,0:T(8,128)S(1)}, bf16[4,1024,128]{2,1,0:T(8,128)(2,1)}, s32[1024,128]{1,0:T(8,128)S(1)}, bf16[4,1024,128]{2,1,0:T(8,128)(2,1)S(1)}, f32[4,1024,128]{2,1,0:T(8,128)S(1)}) custom-call(s32[8,128]{1,0:T(8,128)S(1)} %broadcast_in_dim.9.length_ref, f32[4]{0:T(128)S(1)} %copy-done.3, bf16[528,512]{1,0:T(8,128)(2,1)S(1)} %shard_map.74.high_ref, ...), custom_call_target="tpu_custom_call" | custom-call | flops 7000000000 | bytes 10000000 | tf_op jit(solution)/shard_map/pallas_call | solution.py:228
  16.9 0.0 collective-permute-done.1.got_ref
  17.0 0.0 copy-start.2
  17.0 4.1 %shard_map.76 = (f32[4,1024,128]{2,1,0:T(8,128)S(1)}, f32[2,8,512]{2,1,0:T(8,128)S(1)}) custom-call(s32[8,128]{1,0:T(8,128)S(1)} %broadcast_in_dim.9.length_ref, f32[4]{0:T(128)S(1)} %copy-done.3, bf16[528,512]{1,0:T(8,128)(2,1)S(1)} %collective-permute-done.1.got_ref, bf16[512,2048]{1,0:T(8,128)(2,1)S(1)} %copy-done, ...), custom_call_target="tpu_custom_call" | custom-call | flops 4000000000 | bytes 10000000 | tf_op jit(solution)/shard_map/pallas_call | solution.py:228
  21.1 0.0 collective-permute-done.got_ref
  21.1 0.0 copy-done.2
  21.1 0.0 copy-start.1
  21.1 3.0 %shard_map.77 = f32[16,1,512]{2,1,0:T(1,128)S(1)} custom-call(s32[8,128]{1,0:T(8,128)S(1)} %broadcast_in_dim.9.length_ref, f32[4]{0:T(128)S(1)} %copy-done.3, bf16[528,512]{1,0:T(8,128)(2,1)S(1)} %collective-permute-done.got_ref, bf16[512,2048]{1,0:T(8,128)(2,1)S(1)} %copy-done, s32[1024,128]{1,0:T(8,128)S(1)} %get-tuple-element.13.spread_ref, ...), custom_call_target="tpu_custom_call" | custom-call | flops 2000000000 | bytes 10000000 | tf_op jit(solution)/shard_map/pallas_call | solution.py:228
  24.1 13.6 %all_to_all.20.parts_ref = f32[16,1,512]{2,1,0:T(1,128)S(1)} all-to-all(f32[16,1,512]{2,1,0:T(1,128)S(1)} %shard_map.77), channel_id=1, replica_groups=mesh['hist'=16,'item'=32] {'hist'}, dimensions={0} | all-to-all | bytes 65536 | tf_op jit(solution)/shard_map/all_to_all | solution.py:354
  37.7 0.1 shard_map.78
  37.8 27.6 %all_to_all.21.vecs_ref = f32[32,1,512]{2,1,0:T(1,128)S(1)} all-to-all(f32[32,1,512]{2,1,0:T(1,128)S(1)} %shard_map.78), channel_id=1, replica_groups=mesh['hist'=16,'item'=32] {'item'}, dimensions={0} | all-to-all | bytes 131072 | tf_op jit(solution)/shard_map/all_to_all | solution.py:354
  65.4 0.0 copy-done.1
  65.4 0.7 shard_map.79
  66.1 12.0 %all_to_all.22.parts_ref = f32[16,1,128]{2,1,0:T(1,128)S(1)} all-to-all(f32[16,1,128]{2,1,0:T(1,128)S(1)} %get-tuple-element.19), channel_id=1, replica_groups=mesh['hist'=16,'item'=32] {'hist'}, dimensions={0} | all-to-all | bytes 16384 | tf_op jit(solution)/shard_map/all_to_all | solution.py:354
  78.1 0.1 shard_map.80
  78.2 15.1 %all_to_all.23.parts_ref = f32[32,1,128]{2,1,0:T(1,128)S(1)} all-to-all(f32[32,1,128]{2,1,0:T(1,128)S(1)} %shard_map.80), channel_id=1, replica_groups=mesh['hist'=16,'item'=32] {'item'}, dimensions={0} | all-to-all | bytes 32768 | tf_op jit(solution)/shard_map/all_to_all | solution.py:354
  93.2 0.9 shard_map.81
  (1 shorter events, 0.0 us)
Async XLA Ops:
  1.1 9.9 %copy-start = (bf16[512,2048]{1,0:T(8,128)(2,1)S(1)}, bf16[512,2048]{1,0:T(8,128)(2,1)}, u32[]{:S(2)}) copy-start(bf16[512,2048]{1,0:T(8,128)(2,1)} %w_ref.5) | copy-start | bytes 6291460
  1.1 9.9 %copy-start.3 = (f32[4]{0:T(128)S(1)}, f32[4]{0:T(128)}, u32[]{:S(2)}) copy-start(f32[4]{0:T(128)} %bias_ref.5) | copy-start | bytes 52
  1.1 9.9 %copy-start.4 = (s32[1,1024]{1,0:T(1,128)S(1)}, s32[1,1024]{1,0:T(1,128)}, u32[]{:S(2)}) copy-start(s32[1,1024]{1,0:T(1,128)} %ids_ref.1) | copy-start | bytes 12292
  1.1 15.8 %collective-permute-start.1 = (bf16[528,512]{1,0:T(8,128)(2,1)S(1)}, bf16[528,512]{1,0:T(8,128)(2,1)S(1)}, u32[]{:S(2)}, u32[]{:S(2)}) collective-permute-start(bf16[528,512]{1,0:T(8,128)(2,1)S(1)} %shard_map.74.high_ref), channel_id=1, source_target_pairs={{0,32},{32,64},{64,96},{96,128},{128,160},{160,192},{192,224},{224... | collective-permute-start | bytes 1622024 | tf_op jit(solution)/shard_map/ppermute | solution.py:221
  8.3 12.7 %collective-permute-start = (bf16[528,512]{1,0:T(8,128)(2,1)S(1)}, bf16[528,512]{1,0:T(8,128)(2,1)S(1)}, u32[]{:S(2)}, u32[]{:S(2)}) collective-permute-start(bf16[528,512]{1,0:T(8,128)(2,1)S(1)} %shard_map.73.low_ref), channel_id=1, source_target_pairs={{0,32},{32,64},{64,96},{96,128},{128,160},{160,192},{192,224},{224... | collective-permute-start | bytes 1622024 | tf_op jit(solution)/shard_map/ppermute | solution.py:221
  17.0 4.1 %copy-start.2 = (bf16[512,512]{1,0:T(8,128)(2,1)S(1)}, bf16[512,512]{1,0:T(8,128)(2,1)}, u32[]{:S(2)}) copy-start(bf16[512,512]{1,0:T(8,128)(2,1)} %w_out_ref.1) | copy-start | bytes 1572868
  21.1 44.3 %copy-start.1 = (bf16[1024,512]{1,0:T(8,128)(2,1)S(1)}, bf16[1024,512]{1,0:T(8,128)(2,1)}, u32[]{:S(2)}) copy-start(bf16[1024,512]{1,0:T(8,128)(2,1)} %slab_ref.1) | copy-start | bytes 3145732
